TPU v7x, 128 devices: a whole 4x4x4 slice. The times are simulated.
128 devices in a mesh: shot: 4 (over y_lo, core), gx: 4 (over z), gy: 8 (over x, y_hi).
Axes of the slice: x: 4, y: 4 (y_hi: 2, y_lo: 2; y = y_hi * 2 + y_lo), z: 4, core: 2. Of those that a mesh axis runs over, the one named last changes fastest.
Arguments:
- model_tiles: float32 [256, 256, 128], P(('shot', 'gx'), 'gy'), may hold values from 0.2 to 0.45
- owner_map: int32 [16], replicated, may hold values from 0 to 15, each once
- offsets: int32 [4], P('shot'), may hold values from 0 to 12
- field_now: float32 [4, 2, 64, 256, 128], P('shot', None, 'gx', 'gy'), may hold values from -6 to 6
- field_prev: float32 [4, 2, 64, 256, 128], P('shot', None, 'gx', 'gy'), may hold values from -6 to 6
- sources: int32 [4, 2, 3], P('shot'), may hold values from 0 to 255, as said below
- wavelet: float32 [4, 2, 8], P('shot'), may hold values from -6 to 6
- receivers: int32 [4, 256, 3], P('shot'), may hold values from 0 to 255, as said below
Outputs:
- out_now: float32 [4, 2, 64, 256, 128], P('shot', None, 'gx', 'gy')
- out_prev: float32 [4, 2, 64, 256, 128], P('shot', None, 'gx', 'gy')
- traces: float32 [4, 2, 256, 8], P('shot')
Inputs may be any that keep to these rules, and one draw needn't show every extreme that they name: `sources`: each row is a cell of the group's aperture: first entry below 64, second below 256, third below 128. `receivers`: each row is a cell of the group's aperture: first entry below 64, second below 256, third below 128.
All inputs are finite; a program needn't handle non-finite values.
Results may differ from a plain program's by a relative error of at most 0.0003.
Values sent between devices are 32-bit elements; how exact they have to be, the bound alone decides.
A program may use at most 128 MiB of HBM per device.

v0:
```python
import jax
import jax.numpy as jnp
from jax import lax
from jax.sharding import PartitionSpec as P

STEPS = 8


center_weight = -2.5
near_weight = 4.0 / 3.0
far_weight = -1.0 / 12.0
damp_peak = 0.3


def extended_2(cells, sides, width):
    for axis, dim in sides:
        count = lax.axis_size(axis)
        ends = count - 1
        head = lax.slice_in_dim(cells, 0, width, axis=dim)
        tail = lax.slice_in_dim(cells, cells.shape[dim] - width, cells.shape[dim], axis=dim)
        cells = jnp.concatenate(
            [
                lax.ppermute(tail, axis, [(i, (i + 1) % count) for i in range(ends)]),
                cells,
                lax.ppermute(head, axis, [((i + 1) % count, i) for i in range(ends)]),
            ],
            axis=dim,
        )
    return cells


def depth_ahead(field, reach):
    filler = jnp.zeros(field.shape[:-1] + (reach,), field.dtype)
    return jnp.concatenate([field[..., reach:], filler], axis=-1)


def depth_behind(field, reach):
    filler = jnp.zeros(field.shape[:-1] + (reach,), field.dtype)
    return jnp.concatenate([filler, field[..., :-reach]], axis=-1)


def laplace(extended):
    middle = extended[:, 2:-2, 2:-2]
    along_x = (
        center_weight * middle
        + near_weight * (extended[:, 3:-1, 2:-2] + extended[:, 1:-3, 2:-2])
        + far_weight * (extended[:, 4:, 2:-2] + extended[:, :-4, 2:-2])
    )
    along_y = (
        center_weight * middle
        + near_weight * (extended[:, 2:-2, 3:-1] + extended[:, 2:-2, 1:-3])
        + far_weight * (extended[:, 2:-2, 4:] + extended[:, 2:-2, :-4])
    )
    along_z = (
        center_weight * middle
        + near_weight * (depth_ahead(middle, 1) + depth_behind(middle, 1))
        + far_weight * (depth_ahead(middle, 2) + depth_behind(middle, 2))
    )
    return along_x + along_y + along_z


def damping(x_cells, y_cells, width, x_total, y_total):
    x_depth = (
        jnp.maximum(width - jnp.minimum(x_cells + 1, x_total - x_cells), 0).astype(jnp.float32)
        / width
    )
    y_depth = (
        jnp.maximum(width - jnp.minimum(y_cells + 1, y_total - y_cells), 0).astype(jnp.float32)
        / width
    )
    return damp_peak * (x_depth[:, None] * x_depth[:, None] + y_depth[None, :] * y_depth[None, :])


def injection(x_cells, y_cells, z_cells, source_cells, amplitude):
    on_x = (x_cells[None, :] == source_cells[:, 0:1]).astype(jnp.float32)
    on_y = (y_cells[None, :] == source_cells[:, 1:2]).astype(jnp.float32)
    on_z = (z_cells[None, :] == source_cells[:, 2:3]).astype(jnp.float32)
    return (
        amplitude[:, None, None, None]
        * on_x[:, :, None, None]
        * on_y[:, None, :, None]
        * on_z[:, None, None, :]
    )


def advance(extended, previous, coef, damp, inject):
    middle = extended[:, 2:-2, 2:-2]
    return (2.0 * middle - (1.0 - damp) * previous + coef * laplace(extended) + inject) / (
        1.0 + damp
    )


def sample(field, receiver_cells, x_start, y_start):
    size_x, size_y = (field.shape[1], field.shape[2])
    local_x = receiver_cells[:, 0] - x_start
    local_y = receiver_cells[:, 1] - y_start
    inside = (local_x >= 0) & (local_x < size_x) & (local_y >= 0) & (local_y < size_y)
    values = field[
        :, jnp.clip(local_x, 0, size_x - 1), jnp.clip(local_y, 0, size_y - 1), receiver_cells[:, 2]
    ]
    return jnp.where(inside[None, :], values, 0.0)


def local(model_tiles, owner_map, offsets, field_now, field_prev, sources, wavelet, receivers):
    block_x, block_y, depth = model_tiles.shape
    column_index = lax.axis_index("gx")
    row_index = lax.axis_index("gy")
    across = lax.axis_size("gx")
    total_x = block_x * across
    total_y = block_y * lax.axis_size("gy")
    shift_x = offsets[0]
    tile_total = owner_map.shape[0]
    column_ids = jnp.arange(tile_total, dtype=jnp.int32)
    wanted = jnp.sum(jnp.where(column_ids == shift_x + column_index, owner_map, 0))
    piece = lax.all_gather(model_tiles, ("shot", "gx"), axis=0, tiled=True)
    rows = wanted * block_x + jnp.arange(block_x, dtype=jnp.int32)
    inside = (rows >= 0) & (rows < piece.shape[0])
    taken = jnp.take(piece, jnp.clip(rows, 0, piece.shape[0] - 1), axis=0)
    speed = jnp.where(inside[:, None, None], taken, jnp.zeros_like(model_tiles))
    coef = speed * speed
    current = field_now[0]
    previous = field_prev[0]
    source_cells = sources[0]
    amplitudes = wavelet[0]
    receiver_cells = receivers[0]
    x_start = column_index * block_x
    y_start = row_index * block_y
    x_here = x_start + jnp.arange(block_x, dtype=jnp.int32)
    y_here = y_start + jnp.arange(block_y, dtype=jnp.int32)
    z_cells = jnp.arange(depth, dtype=jnp.int32)
    damp = damping(x_here, y_here, block_x, total_x, total_y)[:, :, None]
    recorded = []
    for step in range(STEPS):
        extended = extended_2(current, (("gx", 1), ("gy", 2)), 2)
        inject = injection(x_here, y_here, z_cells, source_cells, amplitudes[:, step])
        fresh = advance(extended, previous, coef, damp, inject)
        recorded.append(sample(fresh, receiver_cells, x_start, y_start))
        previous = current
        current = fresh
    traces = lax.psum(jnp.stack(recorded, axis=-1), ("gx", "gy"))
    return (current[None], previous[None], traces[None])


def solution(mesh):
    return jax.shard_map(
        local,
        mesh=mesh,
        in_specs=(
            P(("shot", "gx"), "gy", None),
            P(),
            P("shot"),
            P("shot", None, "gx", "gy", None),
            P("shot", None, "gx", "gy", None),
            P("shot", None, None),
            P("shot", None, None),
            P("shot", None, None),
        ),
        out_specs=(
            P("shot", None, "gx", "gy", None),
            P("shot", None, "gx", "gy", None),
            P("shot", None, None, None),
        ),
        check_vma=False,
    )
```

profile of v0, /device:TPU:0, one launch (start us, length us, event | category | flops | bytes accessed | tf_op | source)
XLA Modules:
  0.0 552.8 jit_solution(16876477504030605119)
XLA Ops:
  8.8 1.3 collective-permute-start
  10.1 4.5 collective-permute-start.1
  15.3 1.3 fusion.155
  21.3 2.2 fusion.179
  23.5 2.3 fusion.178
  26.9 1.3 collective-permute-start.2
  28.2 6.1 %collective-permute-start.3 = (f32[2,20,2,128]{3,2,1,0:T(2,128)S(1)}, f32[2,20,2,128]{3,2,1,0:T(2,128)S(1)}, u32[]{:S(2)}, u32[]{:S(2)}) collective-permute-start(f32[2,20,2,128]{3,2,1,0:T(2,128)S(1)} %get-tuple-element.57), channel_id=1, source_target_pairs={{0,1},{1,2},{2,3},{3,4},{4,5},{5,6},{6,7},{8,9},{9,10},{10,11},{11... | collective-permute-start | bytes 122888 | tf_op jit(solution)/shard_map/ppermute | solution.py:23
  34.7 1.5 collective-permute-done.3
  36.1 1.4 pad_maximum_fusion
  37.5 24.6 %all-gather.2.cloned.1.call-done = f32[256,32,128]{2,1,0:T(8,128)} async-done(((f32[16,32,128]{2,1,0:T(8,128)}), f32[256,32,128]{2,1,0:T(8,128)}) %all-gather.2.cloned.1.call-update) | async-done | bytes 4194320 | tf_op jit(solution)/shard_map/all_gather | solution.py:115
  62.1 2.7 gather_fusion
  65.0 3.1 fusion.94
  68.1 1.3 collective-permute-start.4
  69.4 4.5 collective-permute-start.5
  76.1 1.3 collective-permute-start.6
  77.4 6.1 %collective-permute-start.7 = (f32[2,20,2,128]{3,2,1,0:T(2,128)S(1)}, f32[2,20,2,128]{3,2,1,0:T(2,128)S(1)}, u32[]{:S(2)}, u32[]{:S(2)}) collective-permute-start(f32[2,20,2,128]{3,2,1,0:T(2,128)S(1)} %get-tuple-element.53), channel_id=1, source_target_pairs={{0,1},{1,2},{2,3},{3,4},{4,5},{5,6},{6,7},{8,9},{9,10},{10,11},{11... | collective-permute-start | bytes 122888 | tf_op jit(solution)/shard_map/ppermute | solution.py:23
  84.4 16.7 %copy.515 = f32[2,16,32,128]{0,3,2,1:T(8,128)} copy(f32[2,16,32,128]{3,2,1,0:T(8,128)S(1)} %fusion.94) | data formatting | bytes 1048576 | tf_op jit(solution)/shard_map/div | solution.py:88
  101.0 3.0 gather_fusion.1
  104.2 2.0 fusion.82
  106.2 1.3 collective-permute-start.8
  107.5 5.0 collective-permute-start.9
  112.9 1.6 collective-permute-done.9
  114.5 1.3 collective-permute-start.10
  115.8 6.5 %collective-permute-start.11 = (f32[2,20,2,128]{3,2,1,0:T(2,128)S(1)}, f32[2,20,2,128]{3,2,1,0:T(2,128)S(1)}, u32[]{:S(2)}, u32[]{:S(2)}) collective-permute-start(f32[2,20,2,128]{3,2,1,0:T(2,128)S(1)} %get-tuple-element.49), channel_id=1, source_target_pairs={{0,1},{1,2},{2,3},{3,4},{4,5},{5,6},{6,7},{8,9},{9,10},{10,11},{11... | collective-permute-start | bytes 122888 | tf_op jit(solution)/shard_map/ppermute | solution.py:23
  123.2 16.7 %copy.516 = f32[2,16,32,128]{0,3,2,1:T(8,128)} copy(f32[2,16,32,128]{3,2,1,0:T(8,128)S(1)} %fusion.82) | data formatting | bytes 1048576 | tf_op jit(solution)/shard_map/div | solution.py:88
  139.9 3.0 gather_fusion.2
  143.1 2.0 fusion.70
  145.1 1.3 collective-permute-start.12
  146.4 4.9 collective-permute-start.13
  151.6 1.6 collective-permute-done.13
  154.5 7.0 %collective-permute-start.15 = (f32[2,20,2,128]{3,2,1,0:T(2,128)S(1)}, f32[2,20,2,128]{3,2,1,0:T(2,128)S(1)}, u32[]{:S(2)}, u32[]{:S(2)}) collective-permute-start(f32[2,20,2,128]{3,2,1,0:T(2,128)S(1)} %get-tuple-element.45), channel_id=1, source_target_pairs={{0,1},{1,2},{2,3},{3,4},{4,5},{5,6},{6,7},{8,9},{9,10},{10,11},{11... | collective-permute-start | bytes 122888 | tf_op jit(solution)/shard_map/ppermute | solution.py:23
  162.5 16.7 %copy.517 = f32[2,16,32,128]{0,3,2,1:T(8,128)} copy(f32[2,16,32,128]{3,2,1,0:T(8,128)S(1)} %fusion.70) | data formatting | bytes 1048576 | tf_op jit(solution)/shard_map/div | solution.py:88
  179.1 3.0 gather_fusion.3
  182.3 2.0 fusion.58
  184.3 1.3 collective-permute-start.16
  185.6 4.9 collective-permute-start.17
  190.8 1.6 collective-permute-done.17
  193.7 7.1 %collective-permute-start.19 = (f32[2,20,2,128]{3,2,1,0:T(2,128)S(1)}, f32[2,20,2,128]{3,2,1,0:T(2,128)S(1)}, u32[]{:S(2)}, u32[]{:S(2)}) collective-permute-start(f32[2,20,2,128]{3,2,1,0:T(2,128)S(1)} %get-tuple-element.41), channel_id=1, source_target_pairs={{0,1},{1,2},{2,3},{3,4},{4,5},{5,6},{6,7},{8,9},{9,10},{10,11},{11... | collective-permute-start | bytes 122888 | tf_op jit(solution)/shard_map/ppermute | solution.py:23
  201.8 16.7 %copy.518 = f32[2,16,32,128]{0,3,2,1:T(8,128)} copy(f32[2,16,32,128]{3,2,1,0:T(8,128)S(1)} %fusion.58) | data formatting | bytes 1048576 | tf_op jit(solution)/shard_map/div | solution.py:88
  218.5 3.0 gather_fusion.4
  221.7 2.0 fusion.46
  223.7 1.3 collective-permute-start.20
  225.0 4.9 collective-permute-start.21
  230.2 1.6 collective-permute-done.21
  233.1 7.0 %collective-permute-start.23 = (f32[2,20,2,128]{3,2,1,0:T(2,128)S(1)}, f32[2,20,2,128]{3,2,1,0:T(2,128)S(1)}, u32[]{:S(2)}, u32[]{:S(2)}) collective-permute-start(f32[2,20,2,128]{3,2,1,0:T(2,128)S(1)} %get-tuple-element.37), channel_id=1, source_target_pairs={{0,1},{1,2},{2,3},{3,4},{4,5},{5,6},{6,7},{8,9},{9,10},{10,11},{11... | collective-permute-start | bytes 122888 | tf_op jit(solution)/shard_map/ppermute | solution.py:23
  241.0 16.7 %copy.519 = f32[2,16,32,128]{0,3,2,1:T(8,128)} copy(f32[2,16,32,128]{3,2,1,0:T(8,128)S(1)} %fusion.46) | data formatting | bytes 1048576 | tf_op jit(solution)/shard_map/div | solution.py:88
  257.7 3.0 gather_fusion.5
  260.9 2.0 fusion.34
  264.2 4.9 collective-permute-start.25
  269.4 1.6 collective-permute-done.25
  272.3 7.0 %collective-permute-start.27 = (f32[2,20,2,128]{3,2,1,0:T(2,128)S(1)}, f32[2,20,2,128]{3,2,1,0:T(2,128)S(1)}, u32[]{:S(2)}, u32[]{:S(2)}) collective-permute-start(f32[2,20,2,128]{3,2,1,0:T(2,128)S(1)} %get-tuple-element.33), channel_id=1, source_target_pairs={{0,1},{1,2},{2,3},{3,4},{4,5},{5,6},{6,7},{8,9},{9,10},{10,11},{11... | collective-permute-start | bytes 122888 | tf_op jit(solution)/shard_map/ppermute | solution.py:23
  280.2 16.7 %copy.520 = f32[2,16,32,128]{0,3,2,1:T(8,128)} copy(f32[2,16,32,128]{3,2,1,0:T(8,128)S(1)} %fusion.34) | data formatting | bytes 1048576 | tf_op jit(solution)/shard_map/div | solution.py:88
  296.9 3.0 gather_fusion.6
  300.1 2.0 fusion.22
  303.4 4.9 collective-permute-start.29
  308.6 1.6 collective-permute-done.29
  311.5 7.2 %collective-permute-start.31 = (f32[2,20,2,128]{3,2,1,0:T(2,128)S(1)}, f32[2,20,2,128]{3,2,1,0:T(2,128)S(1)}, u32[]{:S(2)}, u32[]{:S(2)}) collective-permute-start(f32[2,20,2,128]{3,2,1,0:T(2,128)S(1)} %get-tuple-element.29), channel_id=1, source_target_pairs={{0,1},{1,2},{2,3},{3,4},{4,5},{5,6},{6,7},{8,9},{9,10},{10,11},{11... | collective-permute-start | bytes 122888 | tf_op jit(solution)/shard_map/ppermute | solution.py:23
  319.7 16.7 %copy.521 = f32[2,16,32,128]{0,3,2,1:T(8,128)} copy(f32[2,16,32,128]{3,2,1,0:T(8,128)S(1)} %fusion.22) | data formatting | bytes 1048576 | tf_op jit(solution)/shard_map/div | solution.py:88
  336.3 3.0 gather_fusion.7
  339.5 2.0 fusion.10
  341.5 16.8 %copy.522 = f32[2,16,32,128]{0,3,2,1:T(8,128)} copy(f32[2,16,32,128]{3,2,1,0:T(8,128)S(1)} %fusion.10) | data formatting | bytes 1048576 | tf_op jit(solution)/shard_map/div | solution.py:88
  358.3 2.4 gather_fusion.8
  360.7 1.4 bitcast_select_fusion
  362.8 183.1 %psum.7 = f32[1,2,256,8]{2,3,1,0:T(8,128)} all-reduce(f32[1,2,256,8]{2,3,1,0:T(8,128)S(1)} %bitcast.70), channel_id=1, replica_groups=mesh['shot'=4,'gx'=4,'gy'=8] {'gx','gy'}, use_global_device_ids=true, to_apply=%region_1.2 | all-reduce | flops 4096 | bytes 32768 | tf_op jit(solution)/shard_map/psum | solution.py:140
  (124 shorter events, 28.7 us)
Async XLA Ops:
  7.2 97.1 %copy-start.1 = (f32[1,2,16,32,128]{4,3,2,1,0:T(8,128)S(1)}, f32[1,2,16,32,128]{4,3,2,1,0:T(8,128)}, u32[]{:S(2)}) copy-start(f32[1,2,16,32,128]{4,3,2,1,0:T(8,128)} %param.11) | copy-start | bytes 1572868
  7.2 54.9 %all-gather.2.cloned.1.call-start = ((), (), s32[]{:S(2)}) async-start(), calls=%async_computation | async-start | bytes 4456448 | tf_op jit(solution)/shard_map/all_gather | solution.py:115
  8.8 17.0 %collective-permute-start = (f32[2,2,32,128]{3,2,1,0:T(8,128)S(1)}, f32[2,2,32,128]{3,2,1,0:T(8,128)S(1)}, u32[]{:S(2)}, u32[]{:S(2)}) collective-permute-start(f32[2,2,32,128]{3,2,1,0:T(8,128)S(1)} %get-tuple-element.104), channel_id=1, source_target_pairs={{8,0},{16,8},{24,16},{9,1},{17,9},{25,17},{10,2},{18,10},{26,18},{... | collective-permute-start | bytes 196616 | tf_op jit(solution)/shard_map/ppermute | solution.py:25
  10.1 15.8 %collective-permute-start.1 = (f32[2,2,32,128]{3,2,1,0:T(8,128)S(1)}, f32[2,2,32,128]{3,2,1,0:T(8,128)S(1)}, u32[]{:S(2)}, u32[]{:S(2)}) collective-permute-start(f32[2,2,32,128]{3,2,1,0:T(8,128)S(1)} %get-tuple-element.105), channel_id=1, source_target_pairs={{0,8},{8,16},{16,24},{1,9},{9,17},{17,25},{2,10},{10,18},{18,26},{... | collective-permute-start | bytes 196616 | tf_op jit(solution)/shard_map/ppermute | solution.py:23
  25.8 39.0 %copy-start.3 = (f32[2,2,32,128]{3,2,1,0:T(8,128)}, f32[2,2,32,128]{3,2,1,0:T(8,128)S(1)}, u32[]{:S(2)}) copy-start(f32[2,2,32,128]{3,2,1,0:T(8,128)S(1)} %collective-permute-done) | copy-start | bytes 196612
  25.9 39.0 %copy-start.4 = (f32[2,2,32,128]{3,2,1,0:T(8,128)}, f32[2,2,32,128]{3,2,1,0:T(8,128)S(1)}, u32[]{:S(2)}) copy-start(f32[2,2,32,128]{3,2,1,0:T(8,128)S(1)} %collective-permute-done.1) | copy-start | bytes 196612
  26.9 7.7 %collective-permute-start.2 = (f32[2,20,2,128]{3,2,1,0:T(2,128)S(1)}, f32[2,20,2,128]{3,2,1,0:T(2,128)S(1)}, u32[]{:S(2)}, u32[]{:S(2)}) collective-permute-start(f32[2,20,2,128]{3,2,1,0:T(2,128)S(1)} %get-tuple-element.56), channel_id=1, source_target_pairs={{1,0},{2,1},{3,2},{4,3},{5,4},{6,5},{7,6},{9,8},{10,9},{11,10},{12... | collective-permute-start | bytes 122888 | tf_op jit(solution)/shard_map/ppermute | solution.py:25
  28.2 7.9 %collective-permute-start.3 = (f32[2,20,2,128]{3,2,1,0:T(2,128)S(1)}, f32[2,20,2,128]{3,2,1,0:T(2,128)S(1)}, u32[]{:S(2)}, u32[]{:S(2)}) collective-permute-start(f32[2,20,2,128]{3,2,1,0:T(2,128)S(1)} %get-tuple-element.57), channel_id=1, source_target_pairs={{0,1},{1,2},{2,3},{3,4},{4,5},{5,6},{6,7},{8,9},{9,10},{10,11},{11... | collective-permute-start | bytes 122888 | tf_op jit(solution)/shard_map/ppermute | solution.py:23
  68.1 6.8 %collective-permute-start.4 = (f32[2,2,32,128]{3,2,1,0:T(8,128)S(1)}, f32[2,2,32,128]{3,2,1,0:T(8,128)S(1)}, u32[]{:S(2)}, u32[]{:S(2)}) collective-permute-start(f32[2,2,32,128]{3,2,1,0:T(8,128)S(1)} %get-tuple-element.98), channel_id=1, source_target_pairs={{8,0},{16,8},{24,16},{9,1},{17,9},{25,17},{10,2},{18,10},{26,18},{... | collective-permute-start | bytes 196616 | tf_op jit(solution)/shard_map/ppermute | solution.py:25
  69.4 6.7 %collective-permute-start.5 = (f32[2,2,32,128]{3,2,1,0:T(8,128)S(1)}, f32[2,2,32,128]{3,2,1,0:T(8,128)S(1)}, u32[]{:S(2)}, u32[]{:S(2)}) collective-permute-start(f32[2,2,32,128]{3,2,1,0:T(8,128)S(1)} %get-tuple-element.99), channel_id=1, source_target_pairs={{0,8},{8,16},{16,24},{1,9},{9,17},{17,25},{2,10},{10,18},{18,26},{... | collective-permute-start | bytes 196616 | tf_op jit(solution)/shard_map/ppermute | solution.py:23
  76.0 28.2 %copy-start.11 = (f32[2,2,32,128]{3,2,1,0:T(8,128)}, f32[2,2,32,128]{3,2,1,0:T(8,128)S(1)}, u32[]{:S(2)}) copy-start(f32[2,2,32,128]{3,2,1,0:T(8,128)S(1)} %collective-permute-done.5) | copy-start | bytes 196612
  76.1 28.0 %collective-permute-start.6 = (f32[2,20,2,128]{3,2,1,0:T(2,128)S(1)}, f32[2,20,2,128]{3,2,1,0:T(2,128)S(1)}, u32[]{:S(2)}, u32[]{:S(2)}) collective-permute-start(f32[2,20,2,128]{3,2,1,0:T(2,128)S(1)} %get-tuple-element.52), channel_id=1, source_target_pairs={{1,0},{2,1},{3,2},{4,3},{5,4},{6,5},{7,6},{9,8},{10,9},{11,10},{12... | collective-permute-start | bytes 122888 | tf_op jit(solution)/shard_map/ppermute | solution.py:25
  77.4 26.7 %collective-permute-start.7 = (f32[2,20,2,128]{3,2,1,0:T(2,128)S(1)}, f32[2,20,2,128]{3,2,1,0:T(2,128)S(1)}, u32[]{:S(2)}, u32[]{:S(2)}) collective-permute-start(f32[2,20,2,128]{3,2,1,0:T(2,128)S(1)} %get-tuple-element.53), channel_id=1, source_target_pairs={{0,1},{1,2},{2,3},{3,4},{4,5},{5,6},{6,7},{8,9},{9,10},{10,11},{11... | collective-permute-start | bytes 122888 | tf_op jit(solution)/shard_map/ppermute | solution.py:23
  106.2 6.6 %collective-permute-start.8 = (f32[2,2,32,128]{3,2,1,0:T(8,128)S(1)}, f32[2,2,32,128]{3,2,1,0:T(8,128)S(1)}, u32[]{:S(2)}, u32[]{:S(2)}) collective-permute-start(f32[2,2,32,128]{3,2,1,0:T(8,128)S(1)} %get-tuple-element.92), channel_id=1, source_target_pairs={{8,0},{16,8},{24,16},{9,1},{17,9},{25,17},{10,2},{18,10},{26,18},{... | collective-permute-start | bytes 196616 | tf_op jit(solution)/shard_map/ppermute | solution.py:25
  107.5 6.9 %collective-permute-start.9 = (f32[2,2,32,128]{3,2,1,0:T(8,128)S(1)}, f32[2,2,32,128]{3,2,1,0:T(8,128)S(1)}, u32[]{:S(2)}, u32[]{:S(2)}) collective-permute-start(f32[2,2,32,128]{3,2,1,0:T(8,128)S(1)} %get-tuple-element.93), channel_id=1, source_target_pairs={{0,8},{8,16},{16,24},{1,9},{9,17},{17,25},{2,10},{10,18},{18,26},{... | collective-permute-start | bytes 196616 | tf_op jit(solution)/shard_map/ppermute | solution.py:23
  114.4 28.7 %copy-start.6 = (f32[2,2,32,128]{3,2,1,0:T(8,128)}, f32[2,2,32,128]{3,2,1,0:T(8,128)S(1)}, u32[]{:S(2)}) copy-start(f32[2,2,32,128]{3,2,1,0:T(8,128)S(1)} %collective-permute-done.9) | copy-start | bytes 196612
  114.5 28.5 %collective-permute-start.10 = (f32[2,20,2,128]{3,2,1,0:T(2,128)S(1)}, f32[2,20,2,128]{3,2,1,0:T(2,128)S(1)}, u32[]{:S(2)}, u32[]{:S(2)}) collective-permute-start(f32[2,20,2,128]{3,2,1,0:T(2,128)S(1)} %get-tuple-element.48), channel_id=1, source_target_pairs={{1,0},{2,1},{3,2},{4,3},{5,4},{6,5},{7,6},{9,8},{10,9},{11,10},{12... | collective-permute-start | bytes 122888 | tf_op jit(solution)/shard_map/ppermute | solution.py:25
  115.8 27.2 %collective-permute-start.11 = (f32[2,20,2,128]{3,2,1,0:T(2,128)S(1)}, f32[2,20,2,128]{3,2,1,0:T(2,128)S(1)}, u32[]{:S(2)}, u32[]{:S(2)}) collective-permute-start(f32[2,20,2,128]{3,2,1,0:T(2,128)S(1)} %get-tuple-element.49), channel_id=1, source_target_pairs={{0,1},{1,2},{2,3},{3,4},{4,5},{5,6},{6,7},{8,9},{9,10},{10,11},{11... | collective-permute-start | bytes 122888 | tf_op jit(solution)/shard_map/ppermute | solution.py:23
  145.1 6.5 %collective-permute-start.12 = (f32[2,2,32,128]{3,2,1,0:T(8,128)S(1)}, f32[2,2,32,128]{3,2,1,0:T(8,128)S(1)}, u32[]{:S(2)}, u32[]{:S(2)}) collective-permute-start(f32[2,2,32,128]{3,2,1,0:T(8,128)S(1)} %get-tuple-element.86), channel_id=1, source_target_pairs={{8,0},{16,8},{24,16},{9,1},{17,9},{25,17},{10,2},{18,10},{26,18},{... | collective-permute-start | bytes 196616 | tf_op jit(solution)/shard_map/ppermute | solution.py:25
  146.4 6.8 %collective-permute-start.13 = (f32[2,2,32,128]{3,2,1,0:T(8,128)S(1)}, f32[2,2,32,128]{3,2,1,0:T(8,128)S(1)}, u32[]{:S(2)}, u32[]{:S(2)}) collective-permute-start(f32[2,2,32,128]{3,2,1,0:T(8,128)S(1)} %get-tuple-element.87), channel_id=1, source_target_pairs={{0,8},{8,16},{16,24},{1,9},{9,17},{17,25},{2,10},{10,18},{18,26},{... | collective-permute-start | bytes 196616 | tf_op jit(solution)/shard_map/ppermute | solution.py:23
  153.2 29.1 %copy-start.7 = (f32[2,2,32,128]{3,2,1,0:T(8,128)}, f32[2,2,32,128]{3,2,1,0:T(8,128)S(1)}, u32[]{:S(2)}) copy-start(f32[2,2,32,128]{3,2,1,0:T(8,128)S(1)} %collective-permute-done.13) | copy-start | bytes 196612
  153.2 28.9 %collective-permute-start.14 = (f32[2,20,2,128]{3,2,1,0:T(2,128)S(1)}, f32[2,20,2,128]{3,2,1,0:T(2,128)S(1)}, u32[]{:S(2)}, u32[]{:S(2)}) collective-permute-start(f32[2,20,2,128]{3,2,1,0:T(2,128)S(1)} %get-tuple-element.44), channel_id=1, source_target_pairs={{1,0},{2,1},{3,2},{4,3},{5,4},{6,5},{7,6},{9,8},{10,9},{11,10},{12... | collective-permute-start | bytes 122888 | tf_op jit(solution)/shard_map/ppermute | solution.py:25
  154.5 27.6 %collective-permute-start.15 = (f32[2,20,2,128]{3,2,1,0:T(2,128)S(1)}, f32[2,20,2,128]{3,2,1,0:T(2,128)S(1)}, u32[]{:S(2)}, u32[]{:S(2)}) collective-permute-start(f32[2,20,2,128]{3,2,1,0:T(2,128)S(1)} %get-tuple-element.45), channel_id=1, source_target_pairs={{0,1},{1,2},{2,3},{3,4},{4,5},{5,6},{6,7},{8,9},{9,10},{10,11},{11... | collective-permute-start | bytes 122888 | tf_op jit(solution)/shard_map/ppermute | solution.py:23
  184.3 6.5 %collective-permute-start.16 = (f32[2,2,32,128]{3,2,1,0:T(8,128)S(1)}, f32[2,2,32,128]{3,2,1,0:T(8,128)S(1)}, u32[]{:S(2)}, u32[]{:S(2)}) collective-permute-start(f32[2,2,32,128]{3,2,1,0:T(8,128)S(1)} %get-tuple-element.80), channel_id=1, source_target_pairs={{8,0},{16,8},{24,16},{9,1},{17,9},{25,17},{10,2},{18,10},{26,18},{... | collective-permute-start | bytes 196616 | tf_op jit(solution)/shard_map/ppermute | solution.py:25
  185.6 6.8 %collective-permute-start.17 = (f32[2,2,32,128]{3,2,1,0:T(8,128)S(1)}, f32[2,2,32,128]{3,2,1,0:T(8,128)S(1)}, u32[]{:S(2)}, u32[]{:S(2)}) collective-permute-start(f32[2,2,32,128]{3,2,1,0:T(8,128)S(1)} %get-tuple-element.81), channel_id=1, source_target_pairs={{0,8},{8,16},{16,24},{1,9},{9,17},{17,25},{2,10},{10,18},{18,26},{... | collective-permute-start | bytes 196616 | tf_op jit(solution)/shard_map/ppermute | solution.py:23
  192.4 29.3 %copy-start.8 = (f32[2,2,32,128]{3,2,1,0:T(8,128)}, f32[2,2,32,128]{3,2,1,0:T(8,128)S(1)}, u32[]{:S(2)}) copy-start(f32[2,2,32,128]{3,2,1,0:T(8,128)S(1)} %collective-permute-done.17) | copy-start | bytes 196612
  192.4 29.1 %collective-permute-start.18 = (f32[2,20,2,128]{3,2,1,0:T(2,128)S(1)}, f32[2,20,2,128]{3,2,1,0:T(2,128)S(1)}, u32[]{:S(2)}, u32[]{:S(2)}) collective-permute-start(f32[2,20,2,128]{3,2,1,0:T(2,128)S(1)} %get-tuple-element.40), channel_id=1, source_target_pairs={{1,0},{2,1},{3,2},{4,3},{5,4},{6,5},{7,6},{9,8},{10,9},{11,10},{12... | collective-permute-start | bytes 122888 | tf_op jit(solution)/shard_map/ppermute | solution.py:25
  193.7 27.8 %collective-permute-start.19 = (f32[2,20,2,128]{3,2,1,0:T(2,128)S(1)}, f32[2,20,2,128]{3,2,1,0:T(2,128)S(1)}, u32[]{:S(2)}, u32[]{:S(2)}) collective-permute-start(f32[2,20,2,128]{3,2,1,0:T(2,128)S(1)} %get-tuple-element.41), channel_id=1, source_target_pairs={{0,1},{1,2},{2,3},{3,4},{4,5},{5,6},{6,7},{8,9},{9,10},{10,11},{11... | collective-permute-start | bytes 122888 | tf_op jit(solution)/shard_map/ppermute | solution.py:23
  223.7 6.5 %collective-permute-start.20 = (f32[2,2,32,128]{3,2,1,0:T(8,128)S(1)}, f32[2,2,32,128]{3,2,1,0:T(8,128)S(1)}, u32[]{:S(2)}, u32[]{:S(2)}) collective-permute-start(f32[2,2,32,128]{3,2,1,0:T(8,128)S(1)} %get-tuple-element.74), channel_id=1, source_target_pairs={{8,0},{16,8},{24,16},{9,1},{17,9},{25,17},{10,2},{18,10},{26,18},{... | collective-permute-start | bytes 196616 | tf_op jit(solution)/shard_map/ppermute | solution.py:25
  225.0 6.8 %collective-permute-start.21 = (f32[2,2,32,128]{3,2,1,0:T(8,128)S(1)}, f32[2,2,32,128]{3,2,1,0:T(8,128)S(1)}, u32[]{:S(2)}, u32[]{:S(2)}) collective-permute-start(f32[2,2,32,128]{3,2,1,0:T(8,128)S(1)} %get-tuple-element.75), channel_id=1, source_target_pairs={{0,8},{8,16},{16,24},{1,9},{9,17},{17,25},{2,10},{10,18},{18,26},{... | collective-permute-start | bytes 196616 | tf_op jit(solution)/shard_map/ppermute | solution.py:23
  231.8 29.1 %copy-start.9 = (f32[2,2,32,128]{3,2,1,0:T(8,128)}, f32[2,2,32,128]{3,2,1,0:T(8,128)S(1)}, u32[]{:S(2)}) copy-start(f32[2,2,32,128]{3,2,1,0:T(8,128)S(1)} %collective-permute-done.21) | copy-start | bytes 196612
  231.8 28.9 %collective-permute-start.22 = (f32[2,20,2,128]{3,2,1,0:T(2,128)S(1)}, f32[2,20,2,128]{3,2,1,0:T(2,128)S(1)}, u32[]{:S(2)}, u32[]{:S(2)}) collective-permute-start(f32[2,20,2,128]{3,2,1,0:T(2,128)S(1)} %get-tuple-element.36), channel_id=1, source_target_pairs={{1,0},{2,1},{3,2},{4,3},{5,4},{6,5},{7,6},{9,8},{10,9},{11,10},{12... | collective-permute-start | bytes 122888 | tf_op jit(solution)/shard_map/ppermute | solution.py:25
  233.1 27.6 %collective-permute-start.23 = (f32[2,20,2,128]{3,2,1,0:T(2,128)S(1)}, f32[2,20,2,128]{3,2,1,0:T(2,128)S(1)}, u32[]{:S(2)}, u32[]{:S(2)}) collective-permute-start(f32[2,20,2,128]{3,2,1,0:T(2,128)S(1)} %get-tuple-element.37), channel_id=1, source_target_pairs={{0,1},{1,2},{2,3},{3,4},{4,5},{5,6},{6,7},{8,9},{9,10},{10,11},{11... | collective-permute-start | bytes 122888 | tf_op jit(solution)/shard_map/ppermute | solution.py:23
  262.9 6.5 %collective-permute-start.24 = (f32[2,2,32,128]{3,2,1,0:T(8,128)S(1)}, f32[2,2,32,128]{3,2,1,0:T(8,128)S(1)}, u32[]{:S(2)}, u32[]{:S(2)}) collective-permute-start(f32[2,2,32,128]{3,2,1,0:T(8,128)S(1)} %get-tuple-element.68), channel_id=1, source_target_pairs={{8,0},{16,8},{24,16},{9,1},{17,9},{25,17},{10,2},{18,10},{26,18},{... | collective-permute-start | bytes 196616 | tf_op jit(solution)/shard_map/ppermute | solution.py:25
  264.2 6.8 %collective-permute-start.25 = (f32[2,2,32,128]{3,2,1,0:T(8,128)S(1)}, f32[2,2,32,128]{3,2,1,0:T(8,128)S(1)}, u32[]{:S(2)}, u32[]{:S(2)}) collective-permute-start(f32[2,2,32,128]{3,2,1,0:T(8,128)S(1)} %get-tuple-element.69), channel_id=1, source_target_pairs={{0,8},{8,16},{16,24},{1,9},{9,17},{17,25},{2,10},{10,18},{18,26},{... | collective-permute-start | bytes 196616 | tf_op jit(solution)/shard_map/ppermute | solution.py:23
  271.0 29.1 %copy-start.10 = (f32[2,2,32,128]{3,2,1,0:T(8,128)}, f32[2,2,32,128]{3,2,1,0:T(8,128)S(1)}, u32[]{:S(2)}) copy-start(f32[2,2,32,128]{3,2,1,0:T(8,128)S(1)} %collective-permute-done.25) | copy-start | bytes 196612
  271.0 28.9 %collective-permute-start.26 = (f32[2,20,2,128]{3,2,1,0:T(2,128)S(1)}, f32[2,20,2,128]{3,2,1,0:T(2,128)S(1)}, u32[]{:S(2)}, u32[]{:S(2)}) collective-permute-start(f32[2,20,2,128]{3,2,1,0:T(2,128)S(1)} %get-tuple-element.32), channel_id=1, source_target_pairs={{1,0},{2,1},{3,2},{4,3},{5,4},{6,5},{7,6},{9,8},{10,9},{11,10},{12... | collective-permute-start | bytes 122888 | tf_op jit(solution)/shard_map/ppermute | solution.py:25
  272.3 27.6 %collective-permute-start.27 = (f32[2,20,2,128]{3,2,1,0:T(2,128)S(1)}, f32[2,20,2,128]{3,2,1,0:T(2,128)S(1)}, u32[]{:S(2)}, u32[]{:S(2)}) collective-permute-start(f32[2,20,2,128]{3,2,1,0:T(2,128)S(1)} %get-tuple-element.33), channel_id=1, source_target_pairs={{0,1},{1,2},{2,3},{3,4},{4,5},{5,6},{6,7},{8,9},{9,10},{10,11},{11... | collective-permute-start | bytes 122888 | tf_op jit(solution)/shard_map/ppermute | solution.py:23
  302.1 56.2 %copy-start = (f32[2,16,32,128]{3,2,1,0:T(8,128)}, f32[2,16,32,128]{3,2,1,0:T(8,128)S(1)}, u32[]{:S(2)}) copy-start(f32[2,16,32,128]{3,2,1,0:T(8,128)S(1)} %fusion.22) | copy-start | bytes 1572868
  302.1 6.5 %collective-permute-start.28 = (f32[2,2,32,128]{3,2,1,0:T(8,128)S(1)}, f32[2,2,32,128]{3,2,1,0:T(8,128)S(1)}, u32[]{:S(2)}, u32[]{:S(2)}) collective-permute-start(f32[2,2,32,128]{3,2,1,0:T(8,128)S(1)} %get-tuple-element.62), channel_id=1, source_target_pairs={{8,0},{16,8},{24,16},{9,1},{17,9},{25,17},{10,2},{18,10},{26,18},{... | collective-permute-start | bytes 196616 | tf_op jit(solution)/shard_map/ppermute | solution.py:25
  303.4 6.8 %collective-permute-start.29 = (f32[2,2,32,128]{3,2,1,0:T(8,128)S(1)}, f32[2,2,32,128]{3,2,1,0:T(8,128)S(1)}, u32[]{:S(2)}, u32[]{:S(2)}) collective-permute-start(f32[2,2,32,128]{3,2,1,0:T(8,128)S(1)} %get-tuple-element.63), channel_id=1, source_target_pairs={{0,8},{8,16},{16,24},{1,9},{9,17},{17,25},{2,10},{10,18},{18,26},{... | collective-permute-start | bytes 196616 | tf_op jit(solution)/shard_map/ppermute | solution.py:23
  310.2 29.3 %copy-start.5 = (f32[2,2,32,128]{3,2,1,0:T(8,128)}, f32[2,2,32,128]{3,2,1,0:T(8,128)S(1)}, u32[]{:S(2)}) copy-start(f32[2,2,32,128]{3,2,1,0:T(8,128)S(1)} %collective-permute-done.29) | copy-start | bytes 196612
  310.2 29.1 %collective-permute-start.30 = (f32[2,20,2,128]{3,2,1,0:T(2,128)S(1)}, f32[2,20,2,128]{3,2,1,0:T(2,128)S(1)}, u32[]{:S(2)}, u32[]{:S(2)}) collective-permute-start(f32[2,20,2,128]{3,2,1,0:T(2,128)S(1)} %get-tuple-element.28), channel_id=1, source_target_pairs={{1,0},{2,1},{3,2},{4,3},{5,4},{6,5},{7,6},{9,8},{10,9},{11,10},{12... | collective-permute-start | bytes 122888 | tf_op jit(solution)/shard_map/ppermute | solution.py:25
  311.5 27.8 %collective-permute-start.31 = (f32[2,20,2,128]{3,2,1,0:T(2,128)S(1)}, f32[2,20,2,128]{3,2,1,0:T(2,128)S(1)}, u32[]{:S(2)}, u32[]{:S(2)}) collective-permute-start(f32[2,20,2,128]{3,2,1,0:T(2,128)S(1)} %get-tuple-element.29), channel_id=1, source_target_pairs={{0,1},{1,2},{2,3},{3,4},{4,5},{5,6},{6,7},{8,9},{9,10},{10,11},{11... | collective-permute-start | bytes 122888 | tf_op jit(solution)/shard_map/ppermute | solution.py:23
  341.5 204.4 %copy-start.2 = (f32[2,16,32,128]{3,2,1,0:T(8,128)}, f32[2,16,32,128]{3,2,1,0:T(8,128)S(1)}, u32[]{:S(2)}) copy-start(f32[2,16,32,128]{3,2,1,0:T(8,128)S(1)} %fusion.10) | copy-start | bytes 1572868
  341.5 19.2 %copy-start.12 = (f32[256,2]{1,0:T(8,128)S(1)}, f32[256,2]{1,0:T(8,128)}, u32[]{:S(2)}) copy-start(f32[256,2]{1,0:T(8,128)} %gather_fusion.7) | copy-start | bytes 6148
Sparse Core Ops, SparseCore 0:
  9.7 52.3 all-gather.1
where the time goes:
time: 554 us; the launch traced here: 553 us
  blocking collectives  183 us (33%)
  local copies, waits for them, and re-layouts  177 us (32%)
  starting transfers between devices  113 us (20%)
  waiting for transfers between devices  39.1 us (7%)
  other arithmetic  24.3 us (4%)
  between operations  16 us (3%)
    psum x1, blocking collectives, local(): traces = lax.psum(jnp.stack(recorded, axis=-1), ('gx', 'gy'))  183 us
    div x8, local copies, waits for them, and re-layouts, advance(): (2.0 * middle - (1.0 - damp) * previous + coef * laplace(extended) + inje...  134 us
    ppermute x16, starting transfers between devices, extended_2(): lax.ppermute(tail, axis, [(i, (i + 1) % count) for i in range(ends)])  92.4 us
    all_gather x1, waiting for transfers between devices, local(): piece = lax.all_gather(model_tiles, ('shot', 'gx'), axis=0, tiled=True)  24.6 us
    gather x8, local copies, waits for them, and re-layouts, sample(): field[:, jnp.clip(local_x, 0, size_x - 1), jnp.clip(local_y, 0, size_y -...  23.5 us
    ppermute x16, starting transfers between devices, extended_2(): lax.ppermute(head, axis, [((i + 1) % count, i) for i in range(ends)])  20.7 us
    div x8, other arithmetic, advance(): (2.0 * middle - (1.0 - damp) * previous + coef * laplace(extended) + inje...  16.9 us
    slice x16, local copies, waits for them, and re-layouts, depth_ahead(): return jnp.concatenate([field[..., reach:], filler], axis=-1)  12.5 us
  transfers between devices with their start and end apart: 33, of which 17 were waited for; matrix products, arithmetic and copies ran while one was open for 29% of the time, Pallas kernels for 0%

commit v1 on v0

v1 whole, which is shorter than its diff:
```python
import jax
import jax.numpy as jnp
from jax import lax
from jax.experimental import pallas as pl
from jax.experimental.pallas import tpu as pltpu
from jax.sharding import PartitionSpec as P

STEPS = 8
SHOTS = 2
NS, NX, NY = 4, 4, 8
GROUP = NS * NX
PEERS = NX * NY
BX, BY, BZ = 16, 32, 128
AX, AY = NX * BX, NY * BY
RECS = 256
PX, PY = BX + 8, BY + 16
X0, Y0 = 4, 8
MESH = pl.DeviceIdType.MESH
F32 = jnp.float32


def loop(n, body, start=0):
    lax.fori_loop(start, n, lambda k, c: (body(k), c)[1], 0)


def kernel(
    tiles, owner, offset, now, prev, sources, wavelet, receivers,
    out_now, out_prev, out_traces,
    U, MT, R, SEL, SELH, EDGE, YM, CO, KC, KA, K2, INV, EY,
    YS, YR, CS, CR, PS, PR, OFS, OFR, OFM, OH, IDL, XB, TS, TR,
    in_sem, off_s, off_r, a_s, a_r, b_s, b_r, bh_s, bh_r, e_s, e_r,
    h_s, h_r, p_s, p_r, t_s, t_r,
):
    s = lax.axis_index("shot")
    i = lax.axis_index("gx")
    j = lax.axis_index("gy")
    me = s * NX + i
    mine = i * NY + j

    def member(d, row):
        return (d // NX, lax.rem(d, NX), row)

    def peer(q):
        return (s, q // NY, lax.rem(q, NY))

    def send(src, dst, ssem, rsem, dev):
        return pltpu.make_async_remote_copy(
            src_ref=src, dst_ref=dst, send_sem=ssem, recv_sem=rsem,
            device_id=dev, device_id_type=MESH,
        )

    inner_x = pl.ds(X0, BX)
    inner_y = pl.ds(Y0, BY)
    has = [i > 0, i < NX - 1, j > 0, j < NY - 1]

    cp_mt = pltpu.make_async_copy(tiles, MT, in_sem.at[0])
    cp_now = pltpu.make_async_copy(now.at[0], U.at[0, :, inner_x, inner_y, :], in_sem.at[1])
    cp_prev = pltpu.make_async_copy(prev.at[0], U.at[2, :, inner_x, inner_y, :], in_sem.at[2])
    cp_mt.start()
    cp_now.start()
    cp_prev.start()

    side_planes = jnp.zeros((4, PY, BZ), F32)
    side_rows = jnp.zeros((8, BZ), F32)
    for b in range(3):
        for sh in range(SHOTS):
            U[b, sh, 0:4] = side_planes
            U[b, sh, PX - 4 : PX] = side_planes

    def zero_rows(x):
        for b in range(3):
            for sh in range(SHOTS):
                U[b, sh, X0 + x, 0:8] = side_rows
                U[b, sh, X0 + x, PY - 8 : PY] = side_rows
        CO[X0 + x, 0:8] = side_rows
        CO[X0 + x, PY - 8 : PY] = side_rows

    loop(BX, zero_rows)
    CO[0:4] = side_planes
    CO[PX - 4 : PX] = side_planes

    barrier = pltpu.get_barrier_semaphore()

    def greet(dev):
        pl.semaphore_signal(barrier, inc=1, device_id=dev, device_id_type=MESH)

    loop(GROUP, lambda r: greet(member(lax.rem(me + r, GROUP), j)), 1)

    @pl.when(has[2])
    def _():
        loop(GROUP, lambda d: greet(member(d, j - 1)))

    @pl.when(has[3])
    def _():
        loop(GROUP, lambda d: greet(member(d, j + 1)))

    def far(row):
        @pl.when((row > j + 1) | (row < j - 1))
        def _():
            for ii in range(NX):
                greet((s, ii, row))

    loop(NY, far)
    near = has[2].astype(jnp.int32) + has[3].astype(jnp.int32)
    pl.semaphore_wait(barrier, GROUP - 1 + GROUP * near + NX * (NY - 1 - near))

    OFS[...] = jnp.full((1, BZ), offset[0], jnp.int32)

    def off_copy(r):
        return send(OFS, OFR.at[s], off_s.at[r], off_r.at[s], (lax.rem(s + r, NS), i, j))

    for r in range(1, NS):
        off_copy(r).start()
    OFR[s] = jnp.full((1, BZ), offset[0], jnp.int32)

    cp_mt.wait()

    def a_copy(r):
        d = lax.rem(me + r, GROUP)
        return send(MT.at[d], R.at[me], a_s.at[r], a_r.at[me], member(d, j))

    loop(GROUP, lambda r: a_copy(r).start(), 1)
    R[me] = MT[me]

    def pack(buf, depth, store):
        def one(x):
            for sh in range(SHOTS):
                store[0, sh * BX + x] = U[buf, sh, X0 + x, pl.ds(Y0, depth)]
                store[1, sh * BX + x] = U[buf, sh, X0 + x, pl.ds(Y0 + BY - depth, depth)]

        loop(BX, one)

    def unpack(buf, depth, store):
        def one(x):
            for sh in range(SHOTS):
                @pl.when(has[2])
                def _():
                    U[buf, sh, X0 + x, pl.ds(Y0 - depth, depth)] = store[0, sh * BX + x]

                @pl.when(has[3])
                def _():
                    U[buf, sh, X0 + x, pl.ds(Y0 + BY, depth)] = store[1, sh * BX + x]

        loop(BX, one)

    corners = [(-1, -1), (-1, 1), (1, -1), (1, 1)]

    def halo_list(buf, slot):
        ends = [pl.ds(X0, 4), pl.ds(X0 + BX - 4, 4)]
        lands = [pl.ds(X0 + BX, 4), pl.ds(X0 - 4, 4)]
        found = []
        for n, dx in ((0, -1), (1, 1)):
            found.append((
                has[n], U.at[buf, :, ends[n], inner_y, :], U.at[buf, :, lands[n], inner_y, :],
                n, 1 - n, (s, i + dx, j),
            ))
        for n, dy in ((0, -1), (1, 1)):
            found.append((
                has[2 + n], YS.at[n], YR.at[slot, 1 - n], 2 + n, 3 - n, (s, i, j + dy),
            ))
        for n, (dx, dy) in enumerate(corners):
            ok = has[0 if dx < 0 else 1] & has[2 if dy < 0 else 3]
            found.append((
                ok, CS.at[n], CR.at[slot, 3 - n], 4 + n, 7 - n, (s, i + dx, j + dy),
            ))
        return found

    def halo_send(buf, slot):
        pack(buf, 4, YS)
        for n, (dx, dy) in enumerate(corners):
            for sh in range(SHOTS):
                for k in range(2):
                    x = X0 + k if dx < 0 else X0 + BX - 2 + k
                    y = Y0 if dy < 0 else Y0 + BY - 2
                    CS[n, sh * 4 + k * 2 : sh * 4 + k * 2 + 2] = U[buf, sh, x, y : y + 2]
        for ok, src, dst, n, m, dev in halo_list(buf, slot):
            @pl.when(ok)
            def _():
                send(src, dst, h_s.at[slot, n], h_r.at[slot, m], dev).start()

    def halo_wait(buf, slot):
        copies = halo_list(buf, slot)
        opposite = [1, 0, 3, 2, 7, 6, 5, 4]
        for n in range(8):
            ok, src, dst, _, m, dev = copies[n]
            back = copies[opposite[n]]

            @pl.when(ok)
            def _():
                send(src, dst, h_s.at[slot, n], h_r.at[slot, m], dev).wait_send()
                send(back[1], back[2], h_s.at[slot, n], h_r.at[slot, n], dev).wait_recv()

        unpack(buf, 4, YR.at[slot])
        for n, (dx, dy) in enumerate(corners):
            @pl.when(copies[4 + n][0])
            def _():
                for sh in range(SHOTS):
                    for k in range(2):
                        x = X0 - 2 + k if dx < 0 else X0 + BX + k
                        y = Y0 - 2 if dy < 0 else Y0 + BY
                        U[buf, sh, x, y : y + 2] = CR[slot, n, sh * 4 + k * 2 : sh * 4 + k * 2 + 2]

    cp_now.wait()
    halo_send(0, 0)
    cp_prev.wait()
    pack(2, 2, PS)
    prev_ends = [pl.ds(X0, 2), pl.ds(X0 + BX - 2, 2)]
    prev_lands = [pl.ds(X0 + BX, 2), pl.ds(X0 - 2, 2)]
    prev_list = []
    for n, dx in ((0, -1), (1, 1)):
        prev_list.append((
            has[n], U.at[2, :, prev_ends[n], inner_y, :], U.at[2, :, prev_lands[n], inner_y, :],
            n, 1 - n, (s, i + dx, j),
        ))
    for n, dy in ((0, -1), (1, 1)):
        prev_list.append((has[2 + n], PS.at[n], PR.at[1 - n], 2 + n, 3 - n, (s, i, j + dy)))
    for ok, src, dst, n, m, dev in prev_list:
        @pl.when(ok)
        def _():
            send(src, dst, p_s.at[n], p_r.at[m], dev).start()

    rows = lax.broadcasted_iota(jnp.int32, (8, BZ), 0)
    lanes = lax.broadcasted_iota(jnp.int32, (8, BZ), 1)
    first_lane = (lanes > 0).astype(F32)
    second_lane = (lanes > 1).astype(F32)
    last_lane = (lanes < BZ - 1).astype(F32)
    last_two = (lanes < BZ - 2).astype(F32)

    def weight(cell, total):
        return jnp.maximum(16 - jnp.minimum(cell + 1, total - cell), 0).astype(F32) / 16.0

    def damping_tables(x):
        wx = weight(jnp.full((8, BZ), i * BX + x - X0, jnp.int32), AX)
        for q in range(5):
            at = pl.ds(Y0 - 4 + 8 * q, 8)
            wy = weight(rows + (j * BY - 4 + 8 * q), AY)
            d = 0.3 * (wx * wx + wy * wy)
            inv = 1.0 / (1.0 + d)
            INV[x, at] = inv
            K2[x, at] = (1.0 - d) * inv

    loop(X0 + BX + 2, damping_tables, X0 - 2)

    for sh in range(SHOTS):
        wx = weight(jnp.full((8, BZ), sources[0, sh, 0], jnp.int32), AX)
        for q in range(5):
            cells = rows + (j * BY - 4 + 8 * q)
            wy = weight(cells, AY)
            inv = 1.0 / (1.0 + 0.3 * (wx * wx + wy * wy))
            hit = (cells == sources[0, sh, 1]) & (lanes == sources[0, sh, 2])
            EY[sh, pl.ds(Y0 - 4 + 8 * q, 8)] = jnp.where(hit, inv, 0.0)

    rx = receivers[0, :, 0:1] - i * BX
    ry = receivers[0, :, 1:2] - j * BY
    rz = receivers[0, :, 2:3]
    here = (rx >= 0) & (rx < BX) & (ry >= 0) & (ry < BY)
    ids = jnp.where(here, rx * BY + ry + 1, 0).astype(F32)
    deep = lax.broadcasted_iota(jnp.int32, (RECS, 2 * BZ), 1)
    deep = jnp.where(deep >= BZ, deep - BZ, deep)
    OH[...] = jnp.where(deep == rz, 1.0, 0.0).astype(jnp.bfloat16)
    square = (RECS, RECS)
    eye = lax.broadcasted_iota(jnp.int32, square, 0) == lax.broadcasted_iota(jnp.int32, square, 1)
    IDL[...] = jnp.sum(jnp.where(eye, ids, 0.0), axis=0, keepdims=True)

    for r in range(1, NS):
        off_copy(r).wait_send()
        other = lax.rem(s + r, NS)
        send(OFS, OFR.at[other], off_s.at[r], off_r.at[other], (other, i, j)).wait_recv()
    cp_off = pltpu.make_async_copy(OFR, OFM, in_sem.at[0])
    cp_off.start()
    cp_off.wait()

    def a_wait(r):
        a_copy(r).wait_send()
        d = lax.rem(me + r, GROUP)
        send(MT.at[d], R.at[d], a_s.at[r], a_r.at[d], member(d, j)).wait_recv()

    loop(GROUP, a_wait, 1)

    tail = me >= GROUP - 2
    head = me < 2
    shift = jnp.where(tail, -1, 1)

    def choose(d):
        column = OFM[d // NX, 0, 0] + lax.rem(d, NX)
        plane = R[owner[column]]
        SEL[d] = plane
        EDGE[0, d] = plane[BY - 2 : BY]
        EDGE[1, d] = plane[0:2]
        SELH[d] = R[owner[jnp.clip(column + shift, 0, GROUP - 1)]]

    loop(GROUP, choose)

    def b_copy(r):
        d = lax.rem(me + r, GROUP)
        return send(
            SEL.at[d], CO.at[X0 + me, inner_y, :], b_s.at[r], b_r.at[me], member(d, j)
        )

    halo_plane = jnp.where(tail, me - (GROUP - 2) + X0 - 2, X0 + BX + jnp.minimum(me, 1))
    halo_slot = jnp.where(tail, me - (GROUP - 2), 2 + jnp.minimum(me, 1))

    def bh_copy(r):
        d = lax.rem(me + r, GROUP)
        return send(
            SELH.at[d], CO.at[halo_plane, inner_y, :], bh_s.at[r], bh_r.at[halo_slot], member(d, j)
        )

    def bh_ok(d):
        c = lax.rem(d, NX)
        return (tail & (c > 0)) | (head & (c < NX - 1))

    def edge_copy(side, d):
        row = j + 1 if side == 0 else j - 1
        return send(
            EDGE.at[side, d], YM.at[side, me], e_s.at[side, d], e_r.at[side, me], member(d, row)
        )

    loop(GROUP, lambda r: b_copy(r).start(), 1)

    def bh_start(r):
        @pl.when(bh_ok(lax.rem(me + r, GROUP)))
        def _():
            bh_copy(r).start()

    loop(GROUP, bh_start, 1)
    for side, ok in ((0, has[3]), (1, has[2])):
        @pl.when(ok)
        def _():
            loop(GROUP, lambda d: edge_copy(side, d).start())

    CO[X0 + me, inner_y] = SEL[me]

    @pl.when(bh_ok(me))
    def _():
        CO[halo_plane, inner_y] = SELH[me]

    halo_wait(0, 0)
    for n in range(4):
        ok, src, dst, _, m, dev = prev_list[n]
        back = prev_list[[1, 0, 3, 2][n]]

        @pl.when(ok)
        def _():
            send(src, dst, p_s.at[n], p_r.at[m], dev).wait_send()
            send(back[1], back[2], p_s.at[n], p_r.at[n], dev).wait_recv()

    unpack(2, 2, PR)

    def b_wait(r):
        b_copy(r).wait_send()
        d = lax.rem(me + r, GROUP)
        send(
            SEL.at[d], CO.at[X0 + d, inner_y, :], b_s.at[r], b_r.at[d], member(d, j)
        ).wait_recv()

        @pl.when(bh_ok(d))
        def _():
            bh_copy(r).wait_send()

    loop(GROUP, b_wait, 1)
    for slot in range(4):
        source = GROUP - 2 + slot if slot < 2 else slot - 2
        plane = X0 - 2 + slot if slot < 2 else X0 + BX + slot - 2
        edge = has[0] if slot < 2 else has[1]

        @pl.when(edge & (me != source))
        def _():
            send(
                SELH.at[0], CO.at[plane, inner_y, :], bh_s.at[0], bh_r.at[slot], member(source, j)
            ).wait_recv()

    for side, to, back in ((0, has[3], has[2]), (1, has[2], has[3])):
        @pl.when(to)
        def _():
            loop(GROUP, lambda d: edge_copy(side, d).wait_send())

        @pl.when(back)
        def _():
            row = j - 1 if side == 0 else j + 1

            def one(d):
                send(
                    EDGE.at[side, d], YM.at[side, d], e_s.at[side, d], e_r.at[side, d],
                    member(d, row),
                ).wait_recv()

            loop(GROUP, one)

            def put(x):
                CO[X0 + x, pl.ds(Y0 - 2 if side == 0 else Y0 + BY, 2)] = YM[side, x]

            loop(BX, put)

    def model_tables(x):
        for q in range(5):
            at = pl.ds(Y0 - 4 + 8 * q, 8)
            speed = CO[x, at]
            inv = INV[x, at]
            scaled = speed * speed * inv
            KC[x, at] = 2.0 * inv - 7.5 * scaled
            KA[x, at] = (4.0 / 3.0) * scaled

    loop(X0 + BX + 2, model_tables, X0 - 2)

    def advance(read, write_from, write, x_lo, x_hi, y_lo, count, step):
        def plane(x):
            on = [
                jnp.where(sources[0, sh, 0] == i * BX + x - X0, wavelet[0, sh, step], 0.0)
                for sh in range(SHOTS)
            ]
            for q in range(count):
                y = y_lo + 8 * q
                at = pl.ds(y, 8)
                kc, ka, k2 = KC[x, at], KA[x, at], K2[x, at]
                for sh in range(SHOTS):
                    c = U[read, sh, x, at]
                    a = (U[read, sh, x + 1, at] + U[read, sh, x - 1, at]) + (
                        U[read, sh, x, pl.ds(y + 1, 8)] + U[read, sh, x, pl.ds(y - 1, 8)]
                    )
                    b = (U[read, sh, x + 2, at] + U[read, sh, x - 2, at]) + (
                        U[read, sh, x, pl.ds(y + 2, 8)] + U[read, sh, x, pl.ds(y - 2, 8)]
                    )
                    a = a + (
                        pltpu.roll(c, 1, 1) * first_lane + pltpu.roll(c, BZ - 1, 1) * last_lane
                    )
                    b = b + (
                        pltpu.roll(c, 2, 1) * second_lane + pltpu.roll(c, BZ - 2, 1) * last_two
                    )
                    fresh = (kc * c - k2 * U[write_from, sh, x, at]) + ka * (a - 0.0625 * b)
                    U[write, sh, x, at] = fresh + EY[sh, at] * on[sh]

        loop(x_hi, plane, x_lo)

    def outer_step(even, step):
        advance(even, 2, 2, X0 - 2, X0 + BX + 2, Y0 - 4, 5, step)

    def inner_step(even, odd_out, step):
        advance(2, even, odd_out, X0, X0 + BX, Y0, 4, step)

    row_ids = lax.broadcasted_iota(jnp.int32, (BX * BY, RECS), 0).astype(F32) + 1.0

    def sample(buf, step):
        def split(x):
            for sh in range(SHOTS):
                v = U[buf, sh, X0 + x, inner_y]
                high = v.astype(jnp.bfloat16)
                low = (v - high.astype(F32)).astype(jnp.bfloat16)
                at = pl.ds(pl.multiple_of((sh * BX + x) * BY, BY), BY)
                XB[at, 0:BZ] = high
                XB[at, BZ : 2 * BZ] = low

        loop(BX, split)
        for sh in range(SHOTS):
            picked = lax.dot_general(
                XB[sh * BX * BY : (sh + 1) * BX * BY], OH[...], (((1,), (1,)), ((), ())),
                preferred_element_type=F32,
            )
            got = jnp.sum(jnp.where(row_ids == IDL[...], picked, 0.0), axis=0, keepdims=True)
            TS[step, 2 * sh : 2 * sh + 1] = got[:, 0:128]
            TS[step, 2 * sh + 1 : 2 * sh + 2] = got[:, 128:256]

    def trace_copy(pair, r):
        at = pl.ds(2 * pair, 2)
        return send(
            TS.at[at], TR.at[mine, at], t_s.at[pair, r], t_r.at[pair, mine],
            peer(lax.rem(mine + r, PEERS)),
        )

    def trace_wait(pair, r):
        trace_copy(pair, r).wait_send()
        q = lax.rem(mine + r, PEERS)
        at = pl.ds(2 * pair, 2)
        send(TS.at[at], TR.at[q, at], t_s.at[pair, r], t_r.at[pair, q], peer(q)).wait_recv()

    def two_steps(pair):
        even = lax.rem(pair, 2)
        later = 1 - even
        outer_step(even, 2 * pair)
        inner_step(even, later, 2 * pair + 1)
        halo_send(later, later)
        sample(2, 2 * pair)
        sample(later, 2 * pair + 1)
        loop(PEERS, lambda r: trace_copy(pair, r).start(), 1)
        halo_wait(later, later)

    pairs = STEPS // 2
    loop(pairs - 1, two_steps)
    last = pairs - 1
    even = last % 2
    later = 1 - even
    outer_step(even, 2 * last)
    cp_out_prev = pltpu.make_async_copy(
        U.at[2, :, inner_x, inner_y, :], out_prev.at[0], in_sem.at[2]
    )
    cp_out_prev.start()
    inner_step(even, later, 2 * last + 1)
    cp_out_now = pltpu.make_async_copy(
        U.at[later, :, inner_x, inner_y, :], out_now.at[0], in_sem.at[1]
    )
    cp_out_now.start()
    sample(2, 2 * last)
    sample(later, 2 * last + 1)
    loop(PEERS, lambda r: trace_copy(last, r).start(), 1)
    out_traces[...] = TS[...]
    for pair in range(pairs):
        loop(PEERS, lambda r: trace_wait(pair, r), 1)

    def add(r):
        out_traces[...] += TR[lax.rem(mine + r, PEERS)]

    loop(PEERS, add, 1)
    cp_out_prev.wait()
    cp_out_now.wait()


def window(tiles, owner, offset, now, prev, sources, wavelet, receivers):
    any_spec = pl.BlockSpec(memory_space=pl.ANY)
    smem = pl.BlockSpec(memory_space=pltpu.SMEM)
    vmem = pl.BlockSpec(memory_space=pltpu.VMEM)
    buf = pltpu.VMEM
    dma = pltpu.SemaphoreType.DMA
    padded = (PX, PY, BZ)
    out_now, out_prev, traces = pl.pallas_call(
        kernel,
        out_shape=(
            jax.ShapeDtypeStruct(now.shape, F32),
            jax.ShapeDtypeStruct(prev.shape, F32),
            jax.ShapeDtypeStruct((STEPS, 2 * SHOTS, 128), F32),
        ),
        in_specs=[any_spec, smem, smem, any_spec, any_spec, smem, smem, vmem],
        out_specs=(any_spec, any_spec, vmem),
        scratch_shapes=[
            buf((3, SHOTS) + padded, F32),
            buf((BX, BY, BZ), F32),
            buf((GROUP, BY, BZ), F32),
            buf((GROUP, BY, BZ), F32),
            buf((GROUP, BY, BZ), F32),
            buf((2, GROUP, 2, BZ), F32),
            buf((2, GROUP, 2, BZ), F32),
            buf(padded, F32),
            buf(padded, F32),
            buf(padded, F32),
            buf(padded, F32),
            buf(padded, F32),
            buf((SHOTS, PY, BZ), F32),
            buf((2, SHOTS * BX, 4, BZ), F32),
            buf((2, 2, SHOTS * BX, 4, BZ), F32),
            buf((4, 8, BZ), F32),
            buf((2, 4, 8, BZ), F32),
            buf((2, SHOTS * BX, 2, BZ), F32),
            buf((2, SHOTS * BX, 2, BZ), F32),
            buf((1, BZ), jnp.int32),
            buf((NS, 1, BZ), jnp.int32),
            pltpu.SMEM((NS, 1, BZ), jnp.int32),
            buf((RECS, 2 * BZ), jnp.bfloat16),
            buf((1, RECS), F32),
            buf((SHOTS * BX * BY, 2 * BZ), jnp.bfloat16),
            buf((STEPS, 2 * SHOTS, 128), F32),
            buf((PEERS, STEPS, 2 * SHOTS, 128), F32),
            dma((3,)), dma((NS,)), dma((NS,)),
            dma((GROUP,)), dma((GROUP,)), dma((GROUP,)), dma((GROUP,)),
            dma((GROUP,)), dma((4,)), dma((2, GROUP)), dma((2, GROUP)),
            dma((2, 8)), dma((2, 8)), dma((4,)), dma((4,)),
            dma((STEPS // 2, PEERS)), dma((STEPS // 2, PEERS)),
        ],
        compiler_params=pltpu.CompilerParams(collective_id=0, has_side_effects=True),
    )(tiles, owner, offset, now, prev, sources, wavelet, receivers)
    traces = traces.reshape(STEPS, SHOTS, RECS)
    return out_now, out_prev, jnp.transpose(traces, (1, 2, 0))[None]


def solution(mesh):
    return jax.shard_map(
        window,
        mesh=mesh,
        in_specs=(
            P(("shot", "gx"), "gy", None),
            P(),
            P("shot"),
            P("shot", None, "gx", "gy", None),
            P("shot", None, "gx", "gy", None),
            P("shot", None, None),
            P("shot", None, None),
            P("shot", None, None),
        ),
        out_specs=(
            P("shot", None, "gx", "gy", None),
            P("shot", None, "gx", "gy", None),
            P("shot", None, None, None),
        ),
        check_vma=False,
    )
```

time: 554 us -> 151 us (0.27)
  blocking collectives: 183 us -> 0 us
  local copies, waits for them, and re-layouts: 177 us -> 5.55 us
  Pallas kernels: 0 us -> 144 us
  starting transfers between devices: 113 us -> 0 us
  waiting for transfers between devices: 39.1 us -> 0 us
  other arithmetic: 24.3 us -> 0 us
  between operations: 16 us -> 1.29 us
    psum x1 -> x0, blocking collectives: 183 us -> none  [local(): traces = lax.psum(jnp.stack(recorded, axis=-1), ('gx', 'gy'))]
    pallas_call x0 -> x1, Pallas kernels: none -> 144 us  [window(): pl.pallas_call(kernel, out_shape=(jax.ShapeDtypeStruct(now.shape, F32), j...]
    div x8 -> x0, local copies, waits for them, and re-layouts: 134 us -> none  [advance(): (2.0 * middle - (1.0 - damp) * previous + coef * laplace(extended) + inje...]
    ppermute x32 -> x0, starting transfers between devices: 113 us -> none  [the longest x16 92.4 us: extended_2(): lax.ppermute(tail, axis, [(i, (i + 1) % count) for i in range(ends)])]
    gather x9 -> x0, local copies, waits for them, and re-layouts: 26.3 us -> none  [the longest x8 23.5 us: sample(): field[:, jnp.clip(local_x, 0, size_x - 1), jnp.clip(local_y, 0, size_y -...]
    all_gather x1 -> x0, waiting for transfers between devices: 24.6 us -> none  [local(): piece = lax.all_gather(model_tiles, ('shot', 'gx'), axis=0, tiled=True)]
    div x8 -> x0, other arithmetic: 16.9 us -> none  [advance(): (2.0 * middle - (1.0 - damp) * previous + coef * laplace(extended) + inje...]
    slice x26 -> x0, local copies, waits for them, and re-layouts: 15.8 us -> none  [the longest x16 12.5 us: depth_ahead(): return jnp.concatenate([field[..., reach:], filler], axis=-1)]
  transfers between devices with their start and end apart: 33 -> 0, of which waited for: 17 -> 0; matrix products, arithmetic and copies ran while one was open for 29% -> 0% of each run, Pallas kernels for 0% -> 0%
where the time goes in v1:
time: 151 us
  Pallas kernels  144 us (95%)
  local copies, waits for them, and re-layouts  5.55 us (4%)
    pallas_call x1, Pallas kernels, window(): pl.pallas_call(kernel, out_shape=(jax.ShapeDtypeStruct(now.shape, F32), j...  144 us
    unnamed x5, local copies, waits for them, and re-layouts  4.2 us

profile of v1, /device:TPU:0, one launch (start us, length us, event | category | flops | bytes accessed | tf_op | source)
XLA Modules:
  0.0 150.8 jit_solution(8171769627237912323)
XLA Ops:
  1.3 1.5 copy.11.receivers
  2.8 144.0 %shard_map.103 = (f32[1,2,16,32,128]{4,3,2,1,0:T(8,128)}, f32[1,2,16,32,128]{4,3,2,1,0:T(8,128)}, f32[8,4,128]{2,1,0:T(4,128)}) custom-call(f32[16,32,128]{2,1,0:T(8,128)} %tiles.1, s32[16]{0:T(128)} %owner.1, s32[1]{0:T(128)S(6)} %copy.17.offset, f32[1,2,16,32,128]{4,3,2,1,0:T(8,128)} %now.1, f32[1,2,16,32,128]{4,3,2,1,0:T(8,128)} %prev.1, ...), custom_call_target="tpu_custom_call" | custom-call | tf_op jit(solution)/shard_map/pallas_call | solution.py:524
  146.8 0.7 reshape.9
  147.5 0.6 copy.14
  148.1 0.0 copy-start
  148.1 1.9 %copy.18 = f32[1,2,16,32,128]{4,3,2,1,0:T(8,128)} copy(f32[1,2,16,32,128]{4,3,2,1,0:T(8,128)} %get-tuple-element.12) | data formatting | bytes 1048576
  150.0 0.0 copy-done
  150.0 0.8 copy.19
Async XLA Ops:
  148.1 1.9 %copy-start = (f32[1,2,16,32,128]{4,3,2,1,0:T(8,128)S(1)}, f32[1,2,16,32,128]{4,3,2,1,0:T(8,128)}, u32[]{:S(2)}) copy-start(f32[1,2,16,32,128]{4,3,2,1,0:T(8,128)} %get-tuple-element.13) | copy-start | bytes 1572868

commit v2 on v1

--- a/solution.py
+++ b/solution.py
@@ -28,8 +28,8 @@
     out_now, out_prev, out_traces,
     U, MT, R, SEL, SELH, EDGE, YM, CO, KC, KA, K2, INV, EY,
     YS, YR, CS, CR, PS, PR, OFS, OFR, OFM, OH, IDL, XB, TS, TR,
-    in_sem, off_s, off_r, a_s, a_r, b_s, b_r, bh_s, bh_r, e_s, e_r,
-    h_s, h_r, p_s, p_r, t_s, t_r,
+    in_sem, off_s, off_r, a_sem, b_sem, bh_s, bh_r, e_sem,
+    h_s, h_r, p_s, p_r, t_sem,
 ):
     s = lax.axis_index("shot")
     i = lax.axis_index("gx")
@@ -38,10 +38,16 @@
     mine = i * NY + j
 
     def member(d, row):
-        return (d // NX, lax.rem(d, NX), row)
+        return (d >> 2, d & (NX - 1), row)
 
     def peer(q):
-        return (s, q // NY, lax.rem(q, NY))
+        return (s, q >> 3, q & (NY - 1))
+
+    def other(r):
+        return (me + r) & (GROUP - 1)
+
+    def all_of(ref, sem):
+        pltpu.make_async_copy(ref, ref, sem).wait()
 
     def send(src, dst, ssem, rsem, dev):
         return pltpu.make_async_remote_copy(
@@ -84,7 +90,7 @@
     def greet(dev):
         pl.semaphore_signal(barrier, inc=1, device_id=dev, device_id_type=MESH)
 
-    loop(GROUP, lambda r: greet(member(lax.rem(me + r, GROUP), j)), 1)
+    loop(GROUP, lambda r: greet(member(other(r), j)), 1)
 
     @pl.when(has[2])
     def _():
@@ -107,7 +113,7 @@
     OFS[...] = jnp.full((1, BZ), offset[0], jnp.int32)
 
     def off_copy(r):
-        return send(OFS, OFR.at[s], off_s.at[r], off_r.at[s], (lax.rem(s + r, NS), i, j))
+        return send(OFS, OFR.at[s], off_s.at[r], off_r.at[s], ((s + r) & (NS - 1), i, j))
 
     for r in range(1, NS):
         off_copy(r).start()
@@ -115,33 +121,26 @@
 
     cp_mt.wait()
 
-    def a_copy(r):
-        d = lax.rem(me + r, GROUP)
-        return send(MT.at[d], R.at[me], a_s.at[r], a_r.at[me], member(d, j))
-
-    loop(GROUP, lambda r: a_copy(r).start(), 1)
+    def a_start(r):
+        d = other(r)
+        send(MT.at[d], R.at[me], a_sem.at[0], a_sem.at[1], member(d, j)).start()
+
+    loop(GROUP, a_start, 1)
     R[me] = MT[me]
 
     def pack(buf, depth, store):
-        def one(x):
+        for x in range(BX):
             for sh in range(SHOTS):
                 store[0, sh * BX + x] = U[buf, sh, X0 + x, pl.ds(Y0, depth)]
                 store[1, sh * BX + x] = U[buf, sh, X0 + x, pl.ds(Y0 + BY - depth, depth)]
 
-        loop(BX, one)
-
     def unpack(buf, depth, store):
-        def one(x):
-            for sh in range(SHOTS):
-                @pl.when(has[2])
-                def _():
-                    U[buf, sh, X0 + x, pl.ds(Y0 - depth, depth)] = store[0, sh * BX + x]
-
-                @pl.when(has[3])
-                def _():
-                    U[buf, sh, X0 + x, pl.ds(Y0 + BY, depth)] = store[1, sh * BX + x]
-
-        loop(BX, one)
+        for side, y in ((0, Y0 - depth), (1, Y0 + BY)):
+            @pl.when(has[2 + side])
+            def _():
+                for x in range(BX):
+                    for sh in range(SHOTS):
+                        U[buf, sh, X0 + x, pl.ds(y, depth)] = store[side, sh * BX + x]
 
     corners = [(-1, -1), (-1, 1), (1, -1), (1, 1)]
 
@@ -250,84 +249,78 @@
             hit = (cells == sources[0, sh, 1]) & (lanes == sources[0, sh, 2])
             EY[sh, pl.ds(Y0 - 4 + 8 * q, 8)] = jnp.where(hit, inv, 0.0)
 
-    rx = receivers[0, :, 0:1] - i * BX
-    ry = receivers[0, :, 1:2] - j * BY
-    rz = receivers[0, :, 2:3]
+    rx = receivers[0] - i * BX
+    ry = receivers[1] - j * BY
     here = (rx >= 0) & (rx < BX) & (ry >= 0) & (ry < BY)
-    ids = jnp.where(here, rx * BY + ry + 1, 0).astype(F32)
-    deep = lax.broadcasted_iota(jnp.int32, (RECS, 2 * BZ), 1)
-    deep = jnp.where(deep >= BZ, deep - BZ, deep)
-    OH[...] = jnp.where(deep == rz, 1.0, 0.0).astype(jnp.bfloat16)
-    square = (RECS, RECS)
-    eye = lax.broadcasted_iota(jnp.int32, square, 0) == lax.broadcasted_iota(jnp.int32, square, 1)
-    IDL[...] = jnp.sum(jnp.where(eye, ids, 0.0), axis=0, keepdims=True)
+    IDL[...] = jnp.where(here, rx * BY + ry, -1)
+    deep = lax.broadcasted_iota(jnp.int32, (2 * BZ, RECS), 0) & (BZ - 1)
+    OH[...] = jnp.where(deep == receivers[2], 1.0, 0.0).astype(jnp.bfloat16)
 
     for r in range(1, NS):
         off_copy(r).wait_send()
-        other = lax.rem(s + r, NS)
-        send(OFS, OFR.at[other], off_s.at[r], off_r.at[other], (other, i, j)).wait_recv()
+        shot = (s + r) & (NS - 1)
+        send(OFS, OFR.at[shot], off_s.at[r], off_r.at[shot], (shot, i, j)).wait_recv()
     cp_off = pltpu.make_async_copy(OFR, OFM, in_sem.at[0])
     cp_off.start()
     cp_off.wait()
-
-    def a_wait(r):
-        a_copy(r).wait_send()
-        d = lax.rem(me + r, GROUP)
-        send(MT.at[d], R.at[d], a_s.at[r], a_r.at[d], member(d, j)).wait_recv()
-
-    loop(GROUP, a_wait, 1)
+    all_of(MT.at[pl.ds(0, GROUP - 1)], a_sem.at[0])
+    all_of(R.at[pl.ds(0, GROUP - 1)], a_sem.at[1])
 
     tail = me >= GROUP - 2
     head = me < 2
     shift = jnp.where(tail, -1, 1)
-
-    def choose(d):
-        column = OFM[d // NX, 0, 0] + lax.rem(d, NX)
-        plane = R[owner[column]]
+    firsts = [OFM[k, 0, 0] for k in range(NS)]
+    for d in range(GROUP):
+        plane = R[owner[firsts[d // NX] + d % NX]]
         SEL[d] = plane
         EDGE[0, d] = plane[BY - 2 : BY]
         EDGE[1, d] = plane[0:2]
-        SELH[d] = R[owner[jnp.clip(column + shift, 0, GROUP - 1)]]
-
-    loop(GROUP, choose)
-
-    def b_copy(r):
-        d = lax.rem(me + r, GROUP)
-        return send(
-            SEL.at[d], CO.at[X0 + me, inner_y, :], b_s.at[r], b_r.at[me], member(d, j)
-        )
+    for d in range(GROUP):
+        column = jnp.clip(firsts[d // NX] + d % NX + shift, 0, GROUP - 1)
+        SELH[d] = R[owner[column]]
 
     halo_plane = jnp.where(tail, me - (GROUP - 2) + X0 - 2, X0 + BX + jnp.minimum(me, 1))
     halo_slot = jnp.where(tail, me - (GROUP - 2), 2 + jnp.minimum(me, 1))
 
     def bh_copy(r):
-        d = lax.rem(me + r, GROUP)
+        d = other(r)
         return send(
             SELH.at[d], CO.at[halo_plane, inner_y, :], bh_s.at[r], bh_r.at[halo_slot], member(d, j)
         )
 
     def bh_ok(d):
-        c = lax.rem(d, NX)
+        c = d & (NX - 1)
         return (tail & (c > 0)) | (head & (c < NX - 1))
 
-    def edge_copy(side, d):
-        row = j + 1 if side == 0 else j - 1
-        return send(
-            EDGE.at[side, d], YM.at[side, me], e_s.at[side, d], e_r.at[side, me], member(d, row)
-        )
-
-    loop(GROUP, lambda r: b_copy(r).start(), 1)
-
-    def bh_start(r):
-        @pl.when(bh_ok(lax.rem(me + r, GROUP)))
-        def _():
-            bh_copy(r).start()
-
-    loop(GROUP, bh_start, 1)
+    def b_start(r):
+        d = other(r)
+        send(
+            SEL.at[d], CO.at[X0 + me, inner_y, :], b_sem.at[0], b_sem.at[1], member(d, j)
+        ).start()
+
+    loop(GROUP, b_start, 1)
+
+    @pl.when(tail | head)
+    def _():
+        def bh_start(r):
+            @pl.when(bh_ok(other(r)))
+            def _():
+                bh_copy(r).start()
+
+        loop(GROUP, bh_start, 1)
+
     for side, ok in ((0, has[3]), (1, has[2])):
         @pl.when(ok)
         def _():
-            loop(GROUP, lambda d: edge_copy(side, d).start())
+            row = j + 1 if side == 0 else j - 1
+
+            def edge_start(d):
+                send(
+                    EDGE.at[side, d], YM.at[side, me], e_sem.at[0, side], e_sem.at[1, side],
+                    member(d, row),
+                ).start()
+
+            loop(GROUP, edge_start)
 
     CO[X0 + me, inner_y] = SEL[me]
 
@@ -347,18 +340,18 @@
 
     unpack(2, 2, PR)
 
-    def b_wait(r):
-        b_copy(r).wait_send()
-        d = lax.rem(me + r, GROUP)
-        send(
-            SEL.at[d], CO.at[X0 + d, inner_y, :], b_s.at[r], b_r.at[d], member(d, j)
-        ).wait_recv()
-
-        @pl.when(bh_ok(d))
-        def _():
-            bh_copy(r).wait_send()
-
-    loop(GROUP, b_wait, 1)
+    all_of(SEL.at[pl.ds(0, GROUP - 1)], b_sem.at[0])
+    all_of(CO.at[pl.ds(0, GROUP - 1), inner_y, :], b_sem.at[1])
+
+    @pl.when(tail | head)
+    def _():
+        def bh_wait(r):
+            @pl.when(bh_ok(other(r)))
+            def _():
+                bh_copy(r).wait_send()
+
+        loop(GROUP, bh_wait, 1)
+
     for slot in range(4):
         source = GROUP - 2 + slot if slot < 2 else slot - 2
         plane = X0 - 2 + slot if slot < 2 else X0 + BX + slot - 2
@@ -373,24 +366,13 @@
     for side, to, back in ((0, has[3], has[2]), (1, has[2], has[3])):
         @pl.when(to)
         def _():
-            loop(GROUP, lambda d: edge_copy(side, d).wait_send())
+            all_of(EDGE.at[side], e_sem.at[0, side])
 
         @pl.when(back)
         def _():
-            row = j - 1 if side == 0 else j + 1
-
-            def one(d):
-                send(
-                    EDGE.at[side, d], YM.at[side, d], e_s.at[side, d], e_r.at[side, d],
-                    member(d, row),
-                ).wait_recv()
-
-            loop(GROUP, one)
-
-            def put(x):
+            all_of(YM.at[side], e_sem.at[1, side])
+            for x in range(BX):
                 CO[X0 + x, pl.ds(Y0 - 2 if side == 0 else Y0 + BY, 2)] = YM[side, x]
-
-            loop(BX, put)
 
     def model_tables(x):
         for q in range(5):
@@ -404,33 +386,44 @@
     loop(X0 + BX + 2, model_tables, X0 - 2)
 
     def advance(read, write_from, write, x_lo, x_hi, y_lo, count, step):
-        def plane(x):
+        def planes(block):
+            first = x_lo + 4 * block
+            done = []
             on = [
-                jnp.where(sources[0, sh, 0] == i * BX + x - X0, wavelet[0, sh, step], 0.0)
-                for sh in range(SHOTS)
+                [
+                    jnp.where(sources[0, sh, 0] == i * BX + first + k - X0, wavelet[0, sh, step], 0.0)
+                    for sh in range(SHOTS)
+                ]
+                for k in range(4)
             ]
             for q in range(count):
                 y = y_lo + 8 * q
                 at = pl.ds(y, 8)
-                kc, ka, k2 = KC[x, at], KA[x, at], K2[x, at]
-                for sh in range(SHOTS):
-                    c = U[read, sh, x, at]
-                    a = (U[read, sh, x + 1, at] + U[read, sh, x - 1, at]) + (
-                        U[read, sh, x, pl.ds(y + 1, 8)] + U[read, sh, x, pl.ds(y - 1, 8)]
-                    )
-                    b = (U[read, sh, x + 2, at] + U[read, sh, x - 2, at]) + (
-                        U[read, sh, x, pl.ds(y + 2, 8)] + U[read, sh, x, pl.ds(y - 2, 8)]
-                    )
-                    a = a + (
-                        pltpu.roll(c, 1, 1) * first_lane + pltpu.roll(c, BZ - 1, 1) * last_lane
-                    )
-                    b = b + (
-                        pltpu.roll(c, 2, 1) * second_lane + pltpu.roll(c, BZ - 2, 1) * last_two
-                    )
-                    fresh = (kc * c - k2 * U[write_from, sh, x, at]) + ka * (a - 0.0625 * b)
-                    U[write, sh, x, at] = fresh + EY[sh, at] * on[sh]
-
-        loop(x_hi, plane, x_lo)
+                for k in range(4):
+                    x = first + k
+                    kc, ka, k2 = KC[x, at], KA[x, at], K2[x, at]
+                    for sh in range(SHOTS):
+                        c = U[read, sh, x, at]
+                        a = (U[read, sh, x + 1, at] + U[read, sh, x - 1, at]) + (
+                            U[read, sh, x, pl.ds(y + 1, 8)] + U[read, sh, x, pl.ds(y - 1, 8)]
+                        )
+                        b = (U[read, sh, x + 2, at] + U[read, sh, x - 2, at]) + (
+                            U[read, sh, x, pl.ds(y + 2, 8)] + U[read, sh, x, pl.ds(y - 2, 8)]
+                        )
+                        a = a + (
+                            pltpu.roll(c, 1, 1) * first_lane
+                            + pltpu.roll(c, BZ - 1, 1) * last_lane
+                        )
+                        b = b + (
+                            pltpu.roll(c, 2, 1) * second_lane
+                            + pltpu.roll(c, BZ - 2, 1) * last_two
+                        )
+                        fresh = (kc * c - k2 * U[write_from, sh, x, at]) + ka * (a - 0.0625 * b)
+                        done.append((sh, x, at, fresh + EY[sh, at] * on[k][sh]))
+            for sh, x, at, fresh in done:
+                U[write, sh, x, at] = fresh
+
+        loop((x_hi - x_lo) // 4, planes)
 
     def outer_step(even, step):
         advance(even, 2, 2, X0 - 2, X0 + BX + 2, Y0 - 4, 5, step)
@@ -438,40 +431,39 @@
     def inner_step(even, odd_out, step):
         advance(2, even, odd_out, X0, X0 + BX, Y0, 4, step)
 
-    row_ids = lax.broadcasted_iota(jnp.int32, (BX * BY, RECS), 0).astype(F32) + 1.0
-
-    def sample(buf, step):
-        def split(x):
-            for sh in range(SHOTS):
-                v = U[buf, sh, X0 + x, inner_y]
-                high = v.astype(jnp.bfloat16)
-                low = (v - high.astype(F32)).astype(jnp.bfloat16)
-                at = pl.ds(pl.multiple_of((sh * BX + x) * BY, BY), BY)
-                XB[at, 0:BZ] = high
-                XB[at, BZ : 2 * BZ] = low
-
-        loop(BX, split)
+    row_ids = lax.broadcasted_iota(jnp.int32, (BX * BY, RECS), 0)
+
+    def sample(buf, pair, half):
+        def split(block):
+            for k in range(4):
+                for sh in range(SHOTS):
+                    x = 4 * block + k
+                    v = U[buf, sh, X0 + x, inner_y]
+                    high = v.astype(jnp.bfloat16)
+                    low = (v - high.astype(F32)).astype(jnp.bfloat16)
+                    at = pl.ds(pl.multiple_of((sh * BX + x) * BY, BY), BY)
+                    XB[at, 0:BZ] = high
+                    XB[at, BZ : 2 * BZ] = low
+
+        loop(BX // 4, split)
         for sh in range(SHOTS):
-            picked = lax.dot_general(
-                XB[sh * BX * BY : (sh + 1) * BX * BY], OH[...], (((1,), (1,)), ((), ())),
-                preferred_element_type=F32,
+            picked = jnp.dot(
+                XB[sh * BX * BY : (sh + 1) * BX * BY], OH[...], preferred_element_type=F32
             )
             got = jnp.sum(jnp.where(row_ids == IDL[...], picked, 0.0), axis=0, keepdims=True)
-            TS[step, 2 * sh : 2 * sh + 1] = got[:, 0:128]
-            TS[step, 2 * sh + 1 : 2 * sh + 2] = got[:, 128:256]
-
-    def trace_copy(pair, r):
-        at = pl.ds(2 * pair, 2)
-        return send(
-            TS.at[at], TR.at[mine, at], t_s.at[pair, r], t_r.at[pair, mine],
-            peer(lax.rem(mine + r, PEERS)),
-        )
-
-    def trace_wait(pair, r):
-        trace_copy(pair, r).wait_send()
-        q = lax.rem(mine + r, PEERS)
-        at = pl.ds(2 * pair, 2)
-        send(TS.at[at], TR.at[q, at], t_s.at[pair, r], t_r.at[pair, q], peer(q)).wait_recv()
+            row = 4 * half + 2 * sh
+            TS[pair, row : row + 1] = got[:, 0:128]
+            TS[pair, row + 1 : row + 2] = got[:, 128:256]
+
+    def trace_send(pair):
+        def one(r):
+            send(
+                TS.at[pair], TR.at[pair, mine], t_sem.at[0, pair], t_sem.at[1, pair],
+                peer((mine + r) & (PEERS - 1)),
+            ).start()
+
+        loop(PEERS, one, 1)
+        TR[pair, mine] = TS[pair]
 
     def two_steps(pair):
         even = lax.rem(pair, 2)
@@ -479,9 +471,9 @@
         outer_step(even, 2 * pair)
         inner_step(even, later, 2 * pair + 1)
         halo_send(later, later)
-        sample(2, 2 * pair)
-        sample(later, 2 * pair + 1)
-        loop(PEERS, lambda r: trace_copy(pair, r).start(), 1)
+        sample(2, pair, 0)
+        sample(later, pair, 1)
+        trace_send(pair)
         halo_wait(later, later)
 
     pairs = STEPS // 2
@@ -499,17 +491,20 @@
         U.at[later, :, inner_x, inner_y, :], out_now.at[0], in_sem.at[1]
     )
     cp_out_now.start()
-    sample(2, 2 * last)
-    sample(later, 2 * last + 1)
-    loop(PEERS, lambda r: trace_copy(last, r).start(), 1)
-    out_traces[...] = TS[...]
+    sample(2, last, 0)
+    sample(later, last, 1)
+    trace_send(last)
     for pair in range(pairs):
-        loop(PEERS, lambda r: trace_wait(pair, r), 1)
-
-    def add(r):
-        out_traces[...] += TR[lax.rem(mine + r, PEERS)]
-
-    loop(PEERS, add, 1)
+        all_of(TR.at[pair, pl.ds(0, PEERS - 1)], t_sem.at[0, pair])
+        all_of(TR.at[pair, pl.ds(0, PEERS - 1)], t_sem.at[1, pair])
+        total = TR[pair, 0]
+        for q in range(1, PEERS):
+            total = total + TR[pair, q]
+        for row in range(8):
+            half, sh, part = row // 4, (row // 2) % 2, row % 2
+            out_traces[sh, 2 * pair + half : 2 * pair + half + 1, 128 * part : 128 * part + 128] = (
+                total[row : row + 1]
+            )
     cp_out_prev.wait()
     cp_out_now.wait()
 
@@ -526,7 +521,7 @@
         out_shape=(
             jax.ShapeDtypeStruct(now.shape, F32),
             jax.ShapeDtypeStruct(prev.shape, F32),
-            jax.ShapeDtypeStruct((STEPS, 2 * SHOTS, 128), F32),
+            jax.ShapeDtypeStruct((SHOTS, STEPS, RECS), F32),
         ),
         in_specs=[any_spec, smem, smem, any_spec, any_spec, smem, smem, vmem],
         out_specs=(any_spec, any_spec, vmem),
@@ -553,21 +548,18 @@
             buf((1, BZ), jnp.int32),
             buf((NS, 1, BZ), jnp.int32),
             pltpu.SMEM((NS, 1, BZ), jnp.int32),
-            buf((RECS, 2 * BZ), jnp.bfloat16),
-            buf((1, RECS), F32),
+            buf((2 * BZ, RECS), jnp.bfloat16),
+            buf((1, RECS), jnp.int32),
             buf((SHOTS * BX * BY, 2 * BZ), jnp.bfloat16),
-            buf((STEPS, 2 * SHOTS, 128), F32),
-            buf((PEERS, STEPS, 2 * SHOTS, 128), F32),
-            dma((3,)), dma((NS,)), dma((NS,)),
-            dma((GROUP,)), dma((GROUP,)), dma((GROUP,)), dma((GROUP,)),
-            dma((GROUP,)), dma((4,)), dma((2, GROUP)), dma((2, GROUP)),
-            dma((2, 8)), dma((2, 8)), dma((4,)), dma((4,)),
-            dma((STEPS // 2, PEERS)), dma((STEPS // 2, PEERS)),
+            buf((STEPS // 2, 8, 128), F32),
+            buf((STEPS // 2, PEERS, 8, 128), F32),
+            dma((3,)), dma((NS,)), dma((NS,)), dma((2,)), dma((2,)),
+            dma((GROUP,)), dma((4,)), dma((2, 2)),
+            dma((2, 8)), dma((2, 8)), dma((4,)), dma((4,)), dma((2, STEPS // 2)),
         ],
         compiler_params=pltpu.CompilerParams(collective_id=0, has_side_effects=True),
-    )(tiles, owner, offset, now, prev, sources, wavelet, receivers)
-    traces = traces.reshape(STEPS, SHOTS, RECS)
-    return out_now, out_prev, jnp.transpose(traces, (1, 2, 0))[None]
+    )(tiles, owner, offset, now, prev, sources, wavelet, jnp.transpose(receivers, (2, 0, 1)))
+    return out_now, out_prev, jnp.transpose(traces, (0, 2, 1))[None]
 
 
 def solution(mesh):

time: 151 us -> 67.3 us (0.45)
  Pallas kernels: 144 us -> 62.3 us
  local copies, waits for them, and re-layouts: 5.55 us -> 3.33 us
    pallas_call x1, Pallas kernels: 144 us -> 62.3 us  [window(): pl.pallas_call(kernel, out_shape=(jax.ShapeDtypeStruct(now.shape, F32), j...]
    unnamed x5 -> x7, local copies, waits for them, and re-layouts: 4.2 us -> 3.33 us
where the time goes in v2:
time: 67.3 us; the launch traced here: 66.9 us
  Pallas kernels  62.3 us (93%)
  local copies, waits for them, and re-layouts  3.33 us (5%)
  between operations  1.3 us (2%)
    pallas_call x1, Pallas kernels, window(): pl.pallas_call(kernel, out_shape=(jax.ShapeDtypeStruct(now.shape, F32), j...  62.3 us
    unnamed x7, local copies, waits for them, and re-layouts  3.33 us

profile of v2, /device:TPU:0, one launch (start us, length us, event | category | flops | bytes accessed | tf_op | source)
XLA Modules:
  0.0 66.9 jit_solution(13897105994020568545)
XLA Ops:
  1.3 62.3 %shard_map.103 = (f32[1,2,16,32,128]{4,3,2,1,0:T(8,128)}, f32[1,2,16,32,128]{4,3,2,1,0:T(8,128)}, f32[2,8,256]{2,1,0:T(8,128)}) custom-call(f32[16,32,128]{2,1,0:T(8,128)} %tiles.1, s32[16]{0:T(128)} %owner.1, s32[1]{0:T(128)S(6)} %copy.14.offset, f32[1,2,16,32,128]{4,3,2,1,0:T(8,128)} %now.1, f32[1,2,16,32,128]{4,3,2,1,0:T(8,128)} %prev.1, ...), custom_call_target="tpu_custom_call" | custom-call | tf_op jit(solution)/shard_map/pallas_call | solution.py:519
  63.6 0.0 copy-start
  63.6 1.9 %copy.15 = f32[1,2,16,32,128]{4,3,2,1,0:T(8,128)} copy(f32[1,2,16,32,128]{4,3,2,1,0:T(8,128)} %get-tuple-element.12) | data formatting | bytes 1048576
  65.5 0.0 copy-done
  65.5 0.0 copy-start.1
  65.5 0.8 %copy.16 = f32[1,2,16,32,128]{4,3,2,1,0:T(8,128)} copy(f32[1,2,16,32,128]{4,3,2,1,0:T(8,128)S(1)} %copy-done) | data formatting | bytes 1048576
  66.3 0.0 copy-done.1
  66.3 0.6 copy.17
Async XLA Ops:
  63.6 1.9 %copy-start = (f32[1,2,16,32,128]{4,3,2,1,0:T(8,128)S(1)}, f32[1,2,16,32,128]{4,3,2,1,0:T(8,128)}, u32[]{:S(2)}) copy-start(f32[1,2,16,32,128]{4,3,2,1,0:T(8,128)} %get-tuple-element.13) | copy-start | bytes 1572868
  65.5 0.8 %copy-start.1 = (f32[2,8,256]{2,1,0:T(8,128)S(1)}, f32[2,8,256]{2,1,0:T(8,128)}, u32[]{:S(2)}) copy-start(f32[2,8,256]{2,1,0:T(8,128)} %get-tuple-element.8) | copy-start | bytes 49156

commit v3 on v2

v3 whole, which is shorter than its diff:
```python
import jax
import jax.numpy as jnp
from jax import lax
from jax.experimental import pallas as pl
from jax.experimental.pallas import tpu as pltpu
from jax.sharding import PartitionSpec as P

STEPS = 8
SHOTS = 2
NS, NX, NY = 4, 4, 8
GROUP = NS * NX
PEERS = NX * NY
BX, BY, BZ = 16, 32, 128
AX, AY = NX * BX, NY * BY
RECS = 256
PX, PY = BX + 8, BY + 16
X0, Y0 = 4, 8
MESH = pl.DeviceIdType.MESH
F32 = jnp.float32


def loop(n, body, start=0):
    lax.fori_loop(start, n, lambda k, c: (body(k), c)[1], 0)


def kernel(
    tiles, owner, offset, now, prev, sources, wavelet, receivers,
    out_now, out_prev, out_traces,
    E0, E1, O, MT, R, SEL, SELH, EDGE, YM, CO, KC, KA, K2, INV, EY,
    YS, YR, CS, CR, PS, PR, OFS, OFR, OFM, OH, IDL, XB, TS, TR,
    in_sem, off_s, off_r, a_sem, b_sem, bh_s, bh_r, e_sem,
    h_s, h_r, p_s, p_r, t_sem,
):
    s = lax.axis_index("shot")
    i = lax.axis_index("gx")
    j = lax.axis_index("gy")
    me = s * NX + i
    mine = i * NY + j

    def member(r):
        return (s ^ (r >> 2), i ^ (r & 3), j)

    def all_of(ref, sem):
        pltpu.make_async_copy(ref, ref, sem).wait()

    def send(src, dst, ssem, rsem, dev):
        return pltpu.make_async_remote_copy(
            src_ref=src, dst_ref=dst, send_sem=ssem, recv_sem=rsem,
            device_id=dev, device_id_type=MESH,
        )

    inner_x = pl.ds(X0, BX)
    inner_y = pl.ds(Y0, BY)
    has = [i > 0, i < NX - 1, j > 0, j < NY - 1]

    cp_mt = pltpu.make_async_copy(tiles, MT, in_sem.at[0])
    cp_now = pltpu.make_async_copy(now.at[0], E0.at[:, inner_x, inner_y, :], in_sem.at[1])
    cp_prev = pltpu.make_async_copy(prev.at[0], O.at[:, inner_x, inner_y, :], in_sem.at[2])
    cp_mt.start()
    cp_now.start()
    cp_prev.start()

    barrier = pltpu.get_barrier_semaphore()

    def greet(dev):
        pl.semaphore_signal(barrier, inc=1, device_id=dev, device_id_type=MESH)

    for r in range(1, NY):
        greet((s, i, j ^ r))
    for r in range(1, GROUP):
        greet(member(r))
    pl.semaphore_wait(barrier, GROUP + NY - 2)

    OFS[...] = jnp.full((1, BZ), offset[0], jnp.int32)

    def off_copy(r):
        return send(OFS, OFR.at[s], off_s.at[r], off_r.at[s], (s ^ r, i, j))

    for r in range(1, NS):
        off_copy(r).start()
    OFR[s] = jnp.full((1, BZ), offset[0], jnp.int32)

    cp_mt.wait()
    for r in range(1, GROUP):
        send(MT.at[me ^ r], R.at[me], a_sem.at[0], a_sem.at[1], member(r)).start()
    R[me] = MT[me]

    def pack(buf, depth, store):
        for x in range(BX):
            for sh in range(SHOTS):
                store[0, sh * BX + x] = buf[sh, X0 + x, pl.ds(Y0, depth)]
                store[1, sh * BX + x] = buf[sh, X0 + x, pl.ds(Y0 + BY - depth, depth)]

    def unpack(buf, depth, store):
        for side, y in ((0, Y0 - depth), (1, Y0 + BY)):
            @pl.when(has[2 + side])
            def _():
                for x in range(BX):
                    for sh in range(SHOTS):
                        buf[sh, X0 + x, pl.ds(y, depth)] = store[side, sh * BX + x]

    corners = [(-1, -1), (-1, 1), (1, -1), (1, 1)]

    def halo_list(buf, slot):
        ends = [pl.ds(X0, 4), pl.ds(X0 + BX - 4, 4)]
        lands = [pl.ds(X0 + BX, 4), pl.ds(X0 - 4, 4)]
        found = []
        for n, dx in ((0, -1), (1, 1)):
            found.append((
                has[n], buf.at[:, ends[n], inner_y, :], buf.at[:, lands[n], inner_y, :],
                n, 1 - n, (s, i + dx, j),
            ))
        for n, dy in ((0, -1), (1, 1)):
            found.append((
                has[2 + n], YS.at[n], YR.at[slot, 1 - n], 2 + n, 3 - n, (s, i, j + dy),
            ))
        for n, (dx, dy) in enumerate(corners):
            ok = has[0 if dx < 0 else 1] & has[2 if dy < 0 else 3]
            found.append((
                ok, CS.at[n], CR.at[slot, 3 - n], 4 + n, 7 - n, (s, i + dx, j + dy),
            ))
        return found

    def start_some(copies, slot):
        for ok, src, dst, n, m, dev in copies:
            @pl.when(ok)
            def _():
                send(src, dst, h_s.at[slot, n], h_r.at[slot, m], dev).start()

    def send_sides(buf, slot):
        start_some(halo_list(buf, slot)[0:2], slot)

    def send_rows(buf, slot):
        pack(buf, 4, YS)
        start_some(halo_list(buf, slot)[2:4], slot)

    def send_corners(buf, slot):
        for n, (dx, dy) in enumerate(corners):
            for sh in range(SHOTS):
                for k in range(2):
                    x = X0 + k if dx < 0 else X0 + BX - 2 + k
                    y = Y0 if dy < 0 else Y0 + BY - 2
                    CS[n, sh * 4 + k * 2 : sh * 4 + k * 2 + 2] = buf[sh, x, y : y + 2]
        start_some(halo_list(buf, slot)[4:8], slot)

    def halo_wait(buf, slot):
        copies = halo_list(buf, slot)
        opposite = [1, 0, 3, 2, 7, 6, 5, 4]
        for n in range(8):
            ok, src, dst, _, m, dev = copies[n]
            back = copies[opposite[n]]

            @pl.when(ok)
            def _():
                send(src, dst, h_s.at[slot, n], h_r.at[slot, m], dev).wait_send()
                send(back[1], back[2], h_s.at[slot, n], h_r.at[slot, n], dev).wait_recv()

        unpack(buf, 4, YR.at[slot])
        for n, (dx, dy) in enumerate(corners):
            @pl.when(copies[4 + n][0])
            def _():
                for sh in range(SHOTS):
                    for k in range(2):
                        x = X0 - 2 + k if dx < 0 else X0 + BX + k
                        y = Y0 - 2 if dy < 0 else Y0 + BY
                        buf[sh, x, y : y + 2] = CR[slot, n, sh * 4 + k * 2 : sh * 4 + k * 2 + 2]

    cp_now.wait()
    send_rows(E0, 0)
    send_sides(E0, 0)
    cp_prev.wait()
    pack(O, 2, PS)
    prev_ends = [pl.ds(X0, 2), pl.ds(X0 + BX - 2, 2)]
    prev_lands = [pl.ds(X0 + BX, 2), pl.ds(X0 - 2, 2)]
    prev_list = []
    for n, dx in ((0, -1), (1, 1)):
        prev_list.append((
            has[n], O.at[:, prev_ends[n], inner_y, :], O.at[:, prev_lands[n], inner_y, :],
            n, 1 - n, (s, i + dx, j),
        ))
    for n, dy in ((0, -1), (1, 1)):
        prev_list.append((has[2 + n], PS.at[n], PR.at[1 - n], 2 + n, 3 - n, (s, i, j + dy)))
    for ok, src, dst, n, m, dev in prev_list:
        @pl.when(ok)
        def _():
            send(src, dst, p_s.at[n], p_r.at[m], dev).start()

    for n, first in ((0, 0), (1, PX - 4)):
        @pl.when(jnp.logical_not(has[n]))
        def _():
            blank = jnp.zeros((4, PY, BZ), F32)
            for buf in (E0, E1, O):
                for sh in range(SHOTS):
                    buf[sh, first : first + 4] = blank
            CO[first : first + 4] = blank

    for n, first in ((2, 0), (3, PY - 8)):
        @pl.when(jnp.logical_not(has[n]))
        def _():
            blank = jnp.zeros((8, BZ), F32)

            def one(x):
                for buf in (E0, E1, O):
                    for sh in range(SHOTS):
                        buf[sh, x, first : first + 8] = blank
                CO[x, first : first + 8] = blank

            loop(PX, one)

    rows = lax.broadcasted_iota(jnp.int32, (8, BZ), 0)
    lanes = lax.broadcasted_iota(jnp.int32, (8, BZ), 1)
    first_lane = (lanes > 0).astype(F32)
    second_lane = (lanes > 1).astype(F32)
    last_lane = (lanes < BZ - 1).astype(F32)
    last_two = (lanes < BZ - 2).astype(F32)

    def weight(cell, total):
        return jnp.maximum(16 - jnp.minimum(cell + 1, total - cell), 0).astype(F32) / 16.0

    def damping_tables(x):
        wx = weight(jnp.full((8, BZ), i * BX + x - X0, jnp.int32), AX)
        for q in range(5):
            at = pl.ds(Y0 - 4 + 8 * q, 8)
            wy = weight(rows + (j * BY - 4 + 8 * q), AY)
            d = 0.3 * (wx * wx + wy * wy)
            inv = 1.0 / (1.0 + d)
            INV[x, at] = inv
            K2[x, at] = (1.0 - d) * inv

    loop(X0 + BX + 2, damping_tables, X0 - 2)

    for sh in range(SHOTS):
        wx = weight(jnp.full((8, BZ), sources[0, sh, 0], jnp.int32), AX)
        for q in range(5):
            cells = rows + (j * BY - 4 + 8 * q)
            wy = weight(cells, AY)
            inv = 1.0 / (1.0 + 0.3 * (wx * wx + wy * wy))
            hit = (cells == sources[0, sh, 1]) & (lanes == sources[0, sh, 2])
            EY[sh, pl.ds(Y0 - 4 + 8 * q, 8)] = jnp.where(hit, inv, 0.0)

    rx = receivers[0] - i * BX
    ry = receivers[1] - j * BY
    here = (rx >= 0) & (rx < BX) & (ry >= 0) & (ry < BY)
    IDL[...] = jnp.where(here, rx * BY + ry, -1)
    deep = lax.broadcasted_iota(jnp.int32, (2 * BZ, RECS), 0) & (BZ - 1)
    OH[...] = jnp.where(deep == receivers[2], 1.0, 0.0).astype(jnp.bfloat16)

    for r in range(1, NS):
        off_copy(r).wait_send()
        shot = s ^ r
        send(OFS, OFR.at[shot], off_s.at[r], off_r.at[shot], (shot, i, j)).wait_recv()
    cp_off = pltpu.make_async_copy(OFR, OFM, in_sem.at[0])
    cp_off.start()
    cp_off.wait()
    all_of(MT.at[pl.ds(0, GROUP - 1)], a_sem.at[0])
    all_of(R.at[pl.ds(0, GROUP - 1)], a_sem.at[1])

    send_corners(E0, 0)

    tail = me >= GROUP - 2
    head = me < 2
    shift = jnp.where(tail, -1, 1)
    firsts = [OFM[s ^ r, 0, 0] for r in range(NS)]
    columns = [firsts[r >> 2] + (i ^ (r & 3)) for r in range(GROUP)]
    for r in range(GROUP):
        plane = R[owner[columns[r]]]
        SEL[r] = plane
        EDGE[0, r] = plane[BY - 2 : BY]
        EDGE[1, r] = plane[0:2]
    halo_plane = jnp.where(tail, me - (GROUP - 2) + X0 - 2, X0 + BX + jnp.minimum(me, 1))
    halo_slot = jnp.where(tail, me - (GROUP - 2), 2 + jnp.minimum(me, 1))

    def bh_copy(r):
        return send(
            SELH.at[r], CO.at[halo_plane, inner_y, :], bh_s.at[r], bh_r.at[halo_slot], member(r)
        )

    def bh_ok(r):
        c = i ^ (r & 3)
        return (tail & (c > 0)) | (head & (c < NX - 1))

    for r in range(1, GROUP):
        send(SEL.at[r], CO.at[X0 + me, inner_y, :], b_sem.at[0], b_sem.at[1], member(r)).start()

    @pl.when(tail | head)
    def _():
        for r in range(GROUP):
            SELH[r] = R[owner[jnp.clip(columns[r] + shift, 0, GROUP - 1)]]
        for r in range(1, GROUP):
            @pl.when(bh_ok(r))
            def _():
                bh_copy(r).start()

    for side, ok in ((0, has[3]), (1, has[2])):
        @pl.when(ok)
        def _():
            row = j + 1 if side == 0 else j - 1
            for r in range(GROUP):
                send(
                    EDGE.at[side, r], YM.at[side, me], e_sem.at[0, side], e_sem.at[1, side],
                    (s ^ (r >> 2), i ^ (r & 3), row),
                ).start()

    CO[X0 + me, inner_y] = SEL[0]

    @pl.when(bh_ok(0))
    def _():
        CO[halo_plane, inner_y] = SELH[0]

    halo_wait(E0, 0)
    for n in range(4):
        ok, src, dst, _, m, dev = prev_list[n]
        back = prev_list[[1, 0, 3, 2][n]]

        @pl.when(ok)
        def _():
            send(src, dst, p_s.at[n], p_r.at[m], dev).wait_send()
            send(back[1], back[2], p_s.at[n], p_r.at[n], dev).wait_recv()

    unpack(O, 2, PR)

    all_of(SEL.at[pl.ds(0, GROUP - 1)], b_sem.at[0])
    all_of(CO.at[pl.ds(0, GROUP - 1), inner_y, :], b_sem.at[1])

    @pl.when(tail | head)
    def _():
        for r in range(1, GROUP):
            @pl.when(bh_ok(r))
            def _():
                bh_copy(r).wait_send()

    for slot in range(4):
        source = GROUP - 2 + slot if slot < 2 else slot - 2
        plane = X0 - 2 + slot if slot < 2 else X0 + BX + slot - 2
        edge = has[0] if slot < 2 else has[1]

        @pl.when(edge & (me != source))
        def _():
            send(
                SELH.at[0], CO.at[plane, inner_y, :], bh_s.at[0], bh_r.at[slot],
                (source >> 2, source & 3, j),
            ).wait_recv()

    for side, to, back in ((0, has[3], has[2]), (1, has[2], has[3])):
        @pl.when(to)
        def _():
            all_of(EDGE.at[side], e_sem.at[0, side])

        @pl.when(back)
        def _():
            all_of(YM.at[side], e_sem.at[1, side])
            for x in range(BX):
                CO[X0 + x, pl.ds(Y0 - 2 if side == 0 else Y0 + BY, 2)] = YM[side, x]

    def model_tables(x):
        for q in range(5):
            at = pl.ds(Y0 - 4 + 8 * q, 8)
            speed = CO[x, at]
            inv = INV[x, at]
            scaled = speed * speed * inv
            KC[x, at] = 2.0 * inv - 7.5 * scaled
            KA[x, at] = (4.0 / 3.0) * scaled

    loop(X0 + BX + 2, model_tables, X0 - 2)

    def advance(read, before, write, first, stride, blocks, wide, tiles, step, lift=(0, 0)):
        def planes(block):
            x_first = first + stride * block
            for k in range(wide):
                x = x_first + k
                on = [
                    jnp.where(sources[0, sh, 0] == i * BX + x - X0, wavelet[0, sh, step], 0.0)
                    for sh in range(SHOTS)
                ]
                for y in tiles:
                    at = pl.ds(y, 8)
                    kc, ka, k2 = KC[x, at], KA[x, at], K2[x, at]
                    for sh in range(SHOTS):
                        c = read[sh, x, at]
                        a = (read[sh, x + 1, at] + read[sh, x - 1, at]) + (
                            read[sh, x, pl.ds(y + 1, 8)] + read[sh, x, pl.ds(y - 1, 8)]
                        )
                        b = (read[sh, x + 2, at] + read[sh, x - 2, at]) + (
                            read[sh, x, pl.ds(y + 2, 8)] + read[sh, x, pl.ds(y - 2, 8)]
                        )
                        a = a + (
                            pltpu.roll(c, 1, 1) * first_lane
                            + pltpu.roll(c, BZ - 1, 1) * last_lane
                        )
                        b = b + (
                            pltpu.roll(c, 2, 1) * second_lane
                            + pltpu.roll(c, BZ - 2, 1) * last_two
                        )
                        fresh = (kc * c - k2 * before[sh, x, at]) + ka * (a - 0.0625 * b)
                        fresh = fresh + EY[sh, at] * on[sh]
                        write[sh, x - lift[0], pl.ds(y - lift[1], 8)] = fresh

        loop(blocks, planes)

    wide_tiles = [Y0 - 4 + 8 * q for q in range(5)]
    own_tiles = [Y0 + 8 * q for q in range(4)]

    def outer_middle(even, step):
        advance(even, O, O, X0 + 2, 4, 3, 4, wide_tiles[1:4], step)

    def outer_ring(even, step):
        advance(even, O, O, X0 - 2, BX, 2, 4, wide_tiles, step)
        advance(even, O, O, X0 + 2, 4, 3, 4, [wide_tiles[0], wide_tiles[4]], step)

    row_ids = lax.broadcasted_iota(jnp.int32, (BX * BY, RECS), 0)

    def sample(buf, pair, half, corner=(X0, Y0)):
        def split(block):
            for k in range(4):
                for sh in range(SHOTS):
                    x = 4 * block + k
                    v = buf[sh, corner[0] + x, pl.ds(corner[1], BY)]
                    high = v.astype(jnp.bfloat16)
                    low = (v - high.astype(F32)).astype(jnp.bfloat16)
                    at = pl.ds(pl.multiple_of((sh * BX + x) * BY, BY), BY)
                    XB[at, 0:BZ] = high
                    XB[at, BZ : 2 * BZ] = low

        loop(BX // 4, split)
        for sh in range(SHOTS):
            picked = jnp.dot(
                XB[sh * BX * BY : (sh + 1) * BX * BY], OH[...], preferred_element_type=F32
            )
            got = jnp.sum(jnp.where(row_ids == IDL[...], picked, 0.0), axis=0, keepdims=True)
            row = 4 * half + 2 * sh
            TS[pair, row : row + 1] = got[:, 0:128]
            TS[pair, row + 1 : row + 2] = got[:, 128:256]

    def trace_send(pair):
        for r in range(1, PEERS):
            send(
                TS.at[pair], TR.at[pair, mine], t_sem.at[0, pair], t_sem.at[1, pair],
                (s, i ^ (r >> 3), j ^ (r & 7)),
            ).start()
        TR[pair, mine] = TS[pair]

    def trace_sum(pair):
        all_of(TR.at[pair, pl.ds(0, PEERS - 1)], t_sem.at[0, pair])
        all_of(TR.at[pair, pl.ds(0, PEERS - 1)], t_sem.at[1, pair])
        parts = [TR[pair, q] for q in range(PEERS)]
        while len(parts) > 1:
            parts = [a + b for a, b in zip(parts[0::2], parts[1::2])]
        for row in range(8):
            half, sh, part = row // 4, (row // 2) % 2, row % 2
            out_traces[sh, 2 * pair + half : 2 * pair + half + 1, 128 * part : 128 * part + 128] = (
                parts[0][row : row + 1]
            )

    pairs = STEPS // 2
    outer_middle(E0, 0)
    for pair in range(pairs):
        even, later = ((E0, E1), (E1, E0))[pair % 2]
        slot = (pair + 1) % 2
        step = 2 * pair + 1
        outer_ring(even, step - 1)
        if pair < pairs - 1:
            advance(O, even, later, X0, 12, 2, 4, own_tiles, step)
            send_sides(later, slot)
            send_corners(later, slot)
            advance(O, even, later, X0 + 4, 4, 2, 4, [own_tiles[0], own_tiles[3]], step)
            send_rows(later, slot)
            advance(O, even, later, X0 + 4, 4, 2, 4, own_tiles[1:3], step)
            sample(O, pair, 0)
            sample(later, pair, 1)
            trace_send(pair)
            outer_middle(later, step + 1)
            if pair:
                trace_sum(pair - 1)
            halo_wait(later, slot)
        else:
            cp_last = pltpu.make_async_copy(
                O.at[:, inner_x, inner_y, :], out_prev.at[0], in_sem.at[2]
            )
            cp_last.start()
            final = out_now.at[0]
            advance(O, even, final, X0, 4, 4, 4, own_tiles, step, (X0, Y0))
            sample(O, pair, 0)
            sample(final, pair, 1, (0, 0))
            trace_send(pair)
            trace_sum(pair - 1)
            trace_sum(pair)
            cp_last.wait()


def window(tiles, owner, offset, now, prev, sources, wavelet, receivers):
    any_spec = pl.BlockSpec(memory_space=pl.ANY)
    smem = pl.BlockSpec(memory_space=pltpu.SMEM)
    vmem = pl.BlockSpec(memory_space=pltpu.VMEM)
    buf = pltpu.VMEM
    dma = pltpu.SemaphoreType.DMA
    padded = (PX, PY, BZ)
    out_now, out_prev, traces = pl.pallas_call(
        kernel,
        out_shape=(
            pltpu.VMEM(now.shape, F32),
            pltpu.VMEM(prev.shape, F32),
            pltpu.VMEM((SHOTS, STEPS, RECS), F32),
        ),
        in_specs=[any_spec, smem, smem, any_spec, any_spec, smem, smem, vmem],
        out_specs=(vmem, vmem, vmem),
        scratch_shapes=[
            buf((SHOTS,) + padded, F32),
            buf((SHOTS,) + padded, F32),
            buf((SHOTS,) + padded, F32),
            buf((BX, BY, BZ), F32),
            buf((GROUP, BY, BZ), F32),
            buf((GROUP, BY, BZ), F32),
            buf((GROUP, BY, BZ), F32),
            buf((2, GROUP, 2, BZ), F32),
            buf((2, GROUP, 2, BZ), F32),
            buf(padded, F32),
            buf(padded, F32),
            buf(padded, F32),
            buf(padded, F32),
            buf(padded, F32),
            buf((SHOTS, PY, BZ), F32),
            buf((2, SHOTS * BX, 4, BZ), F32),
            buf((2, 2, SHOTS * BX, 4, BZ), F32),
            buf((4, 8, BZ), F32),
            buf((2, 4, 8, BZ), F32),
            buf((2, SHOTS * BX, 2, BZ), F32),
            buf((2, SHOTS * BX, 2, BZ), F32),
            buf((1, BZ), jnp.int32),
            buf((NS, 1, BZ), jnp.int32),
            pltpu.SMEM((NS, 1, BZ), jnp.int32),
            buf((2 * BZ, RECS), jnp.bfloat16),
            buf((1, RECS), jnp.int32),
            buf((SHOTS * BX * BY, 2 * BZ), jnp.bfloat16),
            buf((STEPS // 2, 8, 128), F32),
            buf((STEPS // 2, PEERS, 8, 128), F32),
            dma((3,)), dma((NS,)), dma((NS,)), dma((2,)), dma((2,)),
            dma((GROUP,)), dma((4,)), dma((2, 2)),
            dma((2, 8)), dma((2, 8)), dma((4,)), dma((4,)), dma((2, STEPS // 2)),
        ],
        compiler_params=pltpu.CompilerParams(collective_id=0, has_side_effects=True),
    )(tiles, owner, offset, now, prev, sources, wavelet, jnp.transpose(receivers, (2, 0, 1)))
    return out_now, out_prev, jnp.transpose(traces, (0, 2, 1))[None]


def solution(mesh):
    return jax.shard_map(
        window,
        mesh=mesh,
        in_specs=(
            P(("shot", "gx"), "gy", None),
            P(),
            P("shot"),
            P("shot", None, "gx", "gy", None),
            P("shot", None, "gx", "gy", None),
            P("shot", None, None),
            P("shot", None, None),
            P("shot", None, None),
        ),
        out_specs=(
            P("shot", None, "gx", "gy", None),
            P("shot", None, "gx", "gy", None),
            P("shot", None, None, None),
        ),
        check_vma=False,
    )
```

time: 67.3 us -> 61.8 us (0.918)
  Pallas kernels: 62.3 us -> 58.2 us
  local copies, waits for them, and re-layouts: 3.33 us -> 2.19 us
    pallas_call x1, Pallas kernels: 62.3 us -> 58.2 us  [window(): pl.pallas_call(kernel, out_shape=(pltpu.VMEM(now.shape, F32), pltpu.VMEM(...]
    unnamed x7 -> x3, local copies, waits for them, and re-layouts: 3.33 us -> 2.19 us
where the time goes in v3:
time: 61.8 us; the launch traced here: 61.6 us
  Pallas kernels  58.2 us (94%)
  local copies, waits for them, and re-layouts  2.19 us (4%)
  between operations  1.29 us (2%)
    pallas_call x1, Pallas kernels, window(): pl.pallas_call(kernel, out_shape=(pltpu.VMEM(now.shape, F32), pltpu.VMEM(...  58.2 us
    unnamed x3, local copies, waits for them, and re-layouts  2.19 us

profile of v3, /device:TPU:0, one launch (start us, length us, event | category | flops | bytes accessed | tf_op | source)
XLA Modules:
  0.0 61.6 jit_solution(11752768357596566972)
XLA Ops:
  1.3 58.2 %shard_map.103 = (f32[1,2,16,32,128]{4,3,2,1,0:T(8,128)S(1)}, f32[1,2,16,32,128]{4,3,2,1,0:T(8,128)S(1)}, f32[2,8,256]{2,1,0:T(8,128)S(1)}) custom-call(f32[16,32,128]{2,1,0:T(8,128)} %tiles.1, s32[16]{0:T(128)} %owner.1, s32[1]{0:T(128)S(6)} %copy.17.offset, f32[1,2,16,32,128]{4,3,2,1,0:T(8,128)} %now.1, f32[1,2,16,32,128]{4,3,2,1,0:T(8,128)} %prev.1, ...), custom_call_target="tpu_custom_call" | custom-call | tf_op jit(solution)/shard_map/pallas_call | solution.py:497
  59.4 0.8 %copy.14 = f32[1,2,16,32,128]{4,3,2,1,0:T(8,128)} copy(f32[1,2,16,32,128]{4,3,2,1,0:T(8,128)S(1)} %get-tuple-element.9) | data formatting | bytes 1048576
  60.2 0.6 copy.16
  60.8 0.8 %copy.15 = f32[1,2,16,32,128]{4,3,2,1,0:T(8,128)} copy(f32[1,2,16,32,128]{4,3,2,1,0:T(8,128)S(1)} %get-tuple-element.10) | data formatting | bytes 1048576

commit v4 on v3

--- a/solution.py
+++ b/solution.py
@@ -27,7 +27,7 @@
     tiles, owner, offset, now, prev, sources, wavelet, receivers,
     out_now, out_prev, out_traces,
     E0, E1, O, MT, R, SEL, SELH, EDGE, YM, CO, KC, KA, K2, INV, EY,
-    YS, YR, CS, CR, PS, PR, OFS, OFR, OFM, OH, IDL, XB, TS, TR,
+    YS, YR, CS, CR, PS, PR, OFS, OFR, OFM, OH, IDL, XB, ACC, TS, TR,
     in_sem, off_s, off_r, a_sem, b_sem, bh_s, bh_r, e_sem,
     h_s, h_r, p_s, p_r, t_sem,
 ):
@@ -143,10 +143,10 @@
                     CS[n, sh * 4 + k * 2 : sh * 4 + k * 2 + 2] = buf[sh, x, y : y + 2]
         start_some(halo_list(buf, slot)[4:8], slot)
 
-    def halo_wait(buf, slot):
+    def wait_some(buf, slot, which):
         copies = halo_list(buf, slot)
         opposite = [1, 0, 3, 2, 7, 6, 5, 4]
-        for n in range(8):
+        for n in which:
             ok, src, dst, _, m, dev = copies[n]
             back = copies[opposite[n]]
 
@@ -155,6 +155,9 @@
                 send(src, dst, h_s.at[slot, n], h_r.at[slot, m], dev).wait_send()
                 send(back[1], back[2], h_s.at[slot, n], h_r.at[slot, n], dev).wait_recv()
 
+    def wait_rest(buf, slot):
+        copies = halo_list(buf, slot)
+        wait_some(buf, slot, range(2, 8))
         unpack(buf, 4, YR.at[slot])
         for n, (dx, dy) in enumerate(corners):
             @pl.when(copies[4 + n][0])
@@ -165,6 +168,70 @@
                         y = Y0 - 2 if dy < 0 else Y0 + BY
                         buf[sh, x, y : y + 2] = CR[slot, n, sh * 4 + k * 2 : sh * 4 + k * 2 + 2]
 
+    for n, first in ((0, 0), (1, PX - 4)):
+        @pl.when(jnp.logical_not(has[n]))
+        def _():
+            blank = jnp.zeros((4, PY, BZ), F32)
+            for buf in (E0, E1, O):
+                for sh in range(SHOTS):
+                    buf[sh, first : first + 4] = blank
+            CO[first : first + 4] = blank
+
+    for n, first in ((2, 0), (3, PY - 8)):
+        @pl.when(jnp.logical_not(has[n]))
+        def _():
+            blank = jnp.zeros((8, BZ), F32)
+
+            def one(x):
+                for buf in (E0, E1, O):
+                    for sh in range(SHOTS):
+                        buf[sh, x, first : first + 8] = blank
+                CO[x, first : first + 8] = blank
+
+            loop(PX, one)
+
+    rows = lax.broadcasted_iota(jnp.int32, (8, BZ), 0)
+    lanes = lax.broadcasted_iota(jnp.int32, (8, BZ), 1)
+    first_lane = (lanes > 0).astype(F32)
+    second_lane = (lanes > 1).astype(F32)
+    last_lane = (lanes < BZ - 1).astype(F32)
+    last_two = (lanes < BZ - 2).astype(F32)
+
+    def weight(cell, total):
+        return jnp.maximum(16 - jnp.minimum(cell + 1, total - cell), 0).astype(F32) / 16.0
+
+    def damping_tables(x):
+        wx = weight(jnp.full((8, BZ), i * BX + x - X0, jnp.int32), AX)
+        for q in range(5):
+            at = pl.ds(Y0 - 4 + 8 * q, 8)
+            wy = weight(rows + (j * BY - 4 + 8 * q), AY)
+            d = 0.3 * (wx * wx + wy * wy)
+            inv = 1.0 / (1.0 + d)
+            INV[x, at] = inv
+            K2[x, at] = (1.0 - d) * inv
+
+    loop(X0 + BX + 2, damping_tables, X0 - 2)
+
+    for sh in range(SHOTS):
+        wx = weight(jnp.full((8, BZ), sources[0, sh, 0], jnp.int32), AX)
+        for q in range(5):
+            cells = rows + (j * BY - 4 + 8 * q)
+            wy = weight(cells, AY)
+            inv = 1.0 / (1.0 + 0.3 * (wx * wx + wy * wy))
+            hit = (cells == sources[0, sh, 1]) & (lanes == sources[0, sh, 2])
+            EY[sh, pl.ds(Y0 - 4 + 8 * q, 8)] = jnp.where(hit, inv, 0.0)
+
+    rx = receivers[0] - i * BX
+    ry = receivers[1] - j * BY
+    here = (rx >= 0) & (rx < BX) & (ry >= 0) & (ry < BY)
+    IDL[...] = jnp.where(here, rx * BY + ry, -1)
+    deep = lax.broadcasted_iota(jnp.int32, (2 * BZ, RECS), 0) & (BZ - 1)
+    OH[...] = jnp.where(deep == receivers[2], 1.0, 0.0).astype(jnp.bfloat16)
+
+    for r in range(1, NS):
+        off_copy(r).wait_send()
+        shot = s ^ r
+        send(OFS, OFR.at[shot], off_s.at[r], off_r.at[shot], (shot, i, j)).wait_recv()
     cp_now.wait()
     send_rows(E0, 0)
     send_sides(E0, 0)
@@ -185,70 +252,6 @@
         def _():
             send(src, dst, p_s.at[n], p_r.at[m], dev).start()
 
-    for n, first in ((0, 0), (1, PX - 4)):
-        @pl.when(jnp.logical_not(has[n]))
-        def _():
-            blank = jnp.zeros((4, PY, BZ), F32)
-            for buf in (E0, E1, O):
-                for sh in range(SHOTS):
-                    buf[sh, first : first + 4] = blank
-            CO[first : first + 4] = blank
-
-    for n, first in ((2, 0), (3, PY - 8)):
-        @pl.when(jnp.logical_not(has[n]))
-        def _():
-            blank = jnp.zeros((8, BZ), F32)
-
-            def one(x):
-                for buf in (E0, E1, O):
-                    for sh in range(SHOTS):
-                        buf[sh, x, first : first + 8] = blank
-                CO[x, first : first + 8] = blank
-
-            loop(PX, one)
-
-    rows = lax.broadcasted_iota(jnp.int32, (8, BZ), 0)
-    lanes = lax.broadcasted_iota(jnp.int32, (8, BZ), 1)
-    first_lane = (lanes > 0).astype(F32)
-    second_lane = (lanes > 1).astype(F32)
-    last_lane = (lanes < BZ - 1).astype(F32)
-    last_two = (lanes < BZ - 2).astype(F32)
-
-    def weight(cell, total):
-        return jnp.maximum(16 - jnp.minimum(cell + 1, total - cell), 0).astype(F32) / 16.0
-
-    def damping_tables(x):
-        wx = weight(jnp.full((8, BZ), i * BX + x - X0, jnp.int32), AX)
-        for q in range(5):
-            at = pl.ds(Y0 - 4 + 8 * q, 8)
-            wy = weight(rows + (j * BY - 4 + 8 * q), AY)
-            d = 0.3 * (wx * wx + wy * wy)
-            inv = 1.0 / (1.0 + d)
-            INV[x, at] = inv
-            K2[x, at] = (1.0 - d) * inv
-
-    loop(X0 + BX + 2, damping_tables, X0 - 2)
-
-    for sh in range(SHOTS):
-        wx = weight(jnp.full((8, BZ), sources[0, sh, 0], jnp.int32), AX)
-        for q in range(5):
-            cells = rows + (j * BY - 4 + 8 * q)
-            wy = weight(cells, AY)
-            inv = 1.0 / (1.0 + 0.3 * (wx * wx + wy * wy))
-            hit = (cells == sources[0, sh, 1]) & (lanes == sources[0, sh, 2])
-            EY[sh, pl.ds(Y0 - 4 + 8 * q, 8)] = jnp.where(hit, inv, 0.0)
-
-    rx = receivers[0] - i * BX
-    ry = receivers[1] - j * BY
-    here = (rx >= 0) & (rx < BX) & (ry >= 0) & (ry < BY)
-    IDL[...] = jnp.where(here, rx * BY + ry, -1)
-    deep = lax.broadcasted_iota(jnp.int32, (2 * BZ, RECS), 0) & (BZ - 1)
-    OH[...] = jnp.where(deep == receivers[2], 1.0, 0.0).astype(jnp.bfloat16)
-
-    for r in range(1, NS):
-        off_copy(r).wait_send()
-        shot = s ^ r
-        send(OFS, OFR.at[shot], off_s.at[r], off_r.at[shot], (shot, i, j)).wait_recv()
     cp_off = pltpu.make_async_copy(OFR, OFM, in_sem.at[0])
     cp_off.start()
     cp_off.wait()
@@ -279,6 +282,16 @@
         c = i ^ (r & 3)
         return (tail & (c > 0)) | (head & (c < NX - 1))
 
+    for side, ok in ((0, has[3]), (1, has[2])):
+        @pl.when(ok)
+        def _():
+            row = j + 1 if side == 0 else j - 1
+            for r in range(GROUP):
+                send(
+                    EDGE.at[side, r], YM.at[side, me], e_sem.at[0, side], e_sem.at[1, side],
+                    (s ^ (r >> 2), i ^ (r & 3), row),
+                ).start()
+
     for r in range(1, GROUP):
         send(SEL.at[r], CO.at[X0 + me, inner_y, :], b_sem.at[0], b_sem.at[1], member(r)).start()
 
@@ -291,23 +304,14 @@
             def _():
                 bh_copy(r).start()
 
-    for side, ok in ((0, has[3]), (1, has[2])):
-        @pl.when(ok)
-        def _():
-            row = j + 1 if side == 0 else j - 1
-            for r in range(GROUP):
-                send(
-                    EDGE.at[side, r], YM.at[side, me], e_sem.at[0, side], e_sem.at[1, side],
-                    (s ^ (r >> 2), i ^ (r & 3), row),
-                ).start()
-
     CO[X0 + me, inner_y] = SEL[0]
 
     @pl.when(bh_ok(0))
     def _():
         CO[halo_plane, inner_y] = SELH[0]
 
-    halo_wait(E0, 0)
+    wait_some(E0, 0, range(2))
+    wait_rest(E0, 0)
     for n in range(4):
         ok, src, dst, _, m, dev = prev_list[n]
         back = prev_list[[1, 0, 3, 2][n]]
@@ -363,24 +367,34 @@
 
     loop(X0 + BX + 2, model_tables, X0 - 2)
 
-    def advance(read, before, write, first, stride, blocks, wide, tiles, step, lift=(0, 0)):
+    def advance(
+        read, before, write, first, stride, blocks, wide, tiles, step, lift=(0, 0), beside=None
+    ):
         def planes(block):
             x_first = first + stride * block
-            for k in range(wide):
-                x = x_first + k
-                on = [
-                    jnp.where(sources[0, sh, 0] == i * BX + x - X0, wavelet[0, sh, step], 0.0)
+            on = [
+                [
+                    jnp.where(
+                        sources[0, sh, 0] == i * BX + x_first + k - X0, wavelet[0, sh, step], 0.0
+                    )
                     for sh in range(SHOTS)
                 ]
-                for y in tiles:
-                    at = pl.ds(y, 8)
+                for k in range(wide)
+            ]
+            for y in tiles:
+                at = pl.ds(y, 8)
+                line = [
+                    {d: read[sh, x_first + d, at] for d in range(-2, wide + 2)} for sh in range(SHOTS)
+                ]
+                for k in range(wide):
+                    x = x_first + k
                     kc, ka, k2 = KC[x, at], KA[x, at], K2[x, at]
                     for sh in range(SHOTS):
-                        c = read[sh, x, at]
-                        a = (read[sh, x + 1, at] + read[sh, x - 1, at]) + (
+                        c = line[sh][k]
+                        a = (line[sh][k + 1] + line[sh][k - 1]) + (
                             read[sh, x, pl.ds(y + 1, 8)] + read[sh, x, pl.ds(y - 1, 8)]
                         )
-                        b = (read[sh, x + 2, at] + read[sh, x - 2, at]) + (
+                        b = (line[sh][k + 2] + line[sh][k - 2]) + (
                             read[sh, x, pl.ds(y + 2, 8)] + read[sh, x, pl.ds(y - 2, 8)]
                         )
                         a = a + (
@@ -392,44 +406,65 @@
                             + pltpu.roll(c, BZ - 2, 1) * last_two
                         )
                         fresh = (kc * c - k2 * before[sh, x, at]) + ka * (a - 0.0625 * b)
-                        fresh = fresh + EY[sh, at] * on[sh]
+                        fresh = fresh + EY[sh, at] * on[k][sh]
                         write[sh, x - lift[0], pl.ds(y - lift[1], 8)] = fresh
+            if beside is not None:
+                beside(block)
 
         loop(blocks, planes)
 
     wide_tiles = [Y0 - 4 + 8 * q for q in range(5)]
     own_tiles = [Y0 + 8 * q for q in range(4)]
 
+    ends = [wide_tiles[0], wide_tiles[4]]
+
     def outer_middle(even, step):
         advance(even, O, O, X0 + 2, 4, 3, 4, wide_tiles[1:4], step)
 
-    def outer_ring(even, step):
-        advance(even, O, O, X0 - 2, BX, 2, 4, wide_tiles, step)
-        advance(even, O, O, X0 + 2, 4, 3, 4, [wide_tiles[0], wide_tiles[4]], step)
+    def outer_sides(even, step):
+        advance(even, O, O, X0 - 2, BX, 2, 4, wide_tiles[1:4], step)
+
+    def outer_ends(even, step):
+        advance(even, O, O, X0 - 2, 4, 5, 4, ends, step)
 
     row_ids = lax.broadcasted_iota(jnp.int32, (BX * BY, RECS), 0)
 
+    def split(buf, block, corner):
+        for sh in range(SHOTS):
+            for k in range(4):
+                x = 4 * block + k
+                v = buf[sh, corner[0] + x, pl.ds(corner[1], BY)]
+                high = v.astype(jnp.bfloat16)
+                low = (v - high.astype(F32)).astype(jnp.bfloat16)
+                at = pl.ds(pl.multiple_of((sh * BX + x) * BY, BY), BY)
+                XB[at, 0:BZ] = high
+                XB[at, BZ : 2 * BZ] = low
+
+    def keep(pair, half, sh, got):
+        row = 4 * half + 2 * sh
+        TS[pair, row : row + 1] = got[:, 0:128]
+        TS[pair, row + 1 : row + 2] = got[:, 128:256]
+
     def sample(buf, pair, half, corner=(X0, Y0)):
-        def split(block):
-            for k in range(4):
-                for sh in range(SHOTS):
-                    x = 4 * block + k
-                    v = buf[sh, corner[0] + x, pl.ds(corner[1], BY)]
-                    high = v.astype(jnp.bfloat16)
-                    low = (v - high.astype(F32)).astype(jnp.bfloat16)
-                    at = pl.ds(pl.multiple_of((sh * BX + x) * BY, BY), BY)
-                    XB[at, 0:BZ] = high
-                    XB[at, BZ : 2 * BZ] = low
-
-        loop(BX // 4, split)
+        loop(BX // 4, lambda block: split(buf, block, corner))
         for sh in range(SHOTS):
             picked = jnp.dot(
                 XB[sh * BX * BY : (sh + 1) * BX * BY], OH[...], preferred_element_type=F32
             )
             got = jnp.sum(jnp.where(row_ids == IDL[...], picked, 0.0), axis=0, keepdims=True)
-            row = 4 * half + 2 * sh
-            TS[pair, row : row + 1] = got[:, 0:128]
-            TS[pair, row + 1 : row + 2] = got[:, 128:256]
+            keep(pair, half, sh, got)
+
+    def sample_beside(buf):
+        def some(block):
+            split(buf, block, (X0, Y0))
+            wanted = IDL[...] - 4 * BY * block
+            for sh in range(SHOTS):
+                at = pl.ds(pl.multiple_of((sh * BX + 4 * block) * BY, 4 * BY), 4 * BY)
+                picked = jnp.dot(XB[at], OH[...], preferred_element_type=F32)
+                hit = jnp.where(row_ids[: 4 * BY] == wanted, picked, 0.0)
+                ACC[sh] += jnp.sum(hit.reshape(4 * BY // 8, 8, RECS), axis=0)
+
+        return some
 
     def trace_send(pair):
         for r in range(1, PEERS):
@@ -453,17 +488,18 @@
 
     pairs = STEPS // 2
     outer_middle(E0, 0)
+    outer_sides(E0, 0)
     for pair in range(pairs):
         even, later = ((E0, E1), (E1, E0))[pair % 2]
         slot = (pair + 1) % 2
         step = 2 * pair + 1
-        outer_ring(even, step - 1)
+        outer_ends(even, step - 1)
         if pair < pairs - 1:
-            advance(O, even, later, X0, 12, 2, 4, own_tiles, step)
+            advance(O, even, later, X0, 4, 4, 4, [own_tiles[0], own_tiles[3]], step)
+            send_rows(later, slot)
+            send_corners(later, slot)
+            advance(O, even, later, X0, 12, 2, 4, own_tiles[1:3], step)
             send_sides(later, slot)
-            send_corners(later, slot)
-            advance(O, even, later, X0 + 4, 4, 2, 4, [own_tiles[0], own_tiles[3]], step)
-            send_rows(later, slot)
             advance(O, even, later, X0 + 4, 4, 2, 4, own_tiles[1:3], step)
             sample(O, pair, 0)
             sample(later, pair, 1)
@@ -471,15 +507,21 @@
             outer_middle(later, step + 1)
             if pair:
                 trace_sum(pair - 1)
-            halo_wait(later, slot)
+            wait_some(later, slot, range(2))
+            outer_sides(later, step + 1)
+            wait_rest(later, slot)
         else:
             cp_last = pltpu.make_async_copy(
                 O.at[:, inner_x, inner_y, :], out_prev.at[0], in_sem.at[2]
             )
             cp_last.start()
             final = out_now.at[0]
-            advance(O, even, final, X0, 4, 4, 4, own_tiles, step, (X0, Y0))
-            sample(O, pair, 0)
+            ACC[...] = jnp.zeros_like(ACC)
+            advance(
+                O, even, final, X0, 4, 4, 4, own_tiles, step, (X0, Y0), sample_beside(O)
+            )
+            for sh in range(SHOTS):
+                keep(pair, 0, sh, jnp.sum(ACC[sh], axis=0, keepdims=True))
             sample(final, pair, 1, (0, 0))
             trace_send(pair)
             trace_sum(pair - 1)
@@ -531,6 +573,7 @@
             buf((2 * BZ, RECS), jnp.bfloat16),
             buf((1, RECS), jnp.int32),
             buf((SHOTS * BX * BY, 2 * BZ), jnp.bfloat16),
+            buf((SHOTS, 8, RECS), F32),
             buf((STEPS // 2, 8, 128), F32),
             buf((STEPS // 2, PEERS, 8, 128), F32),
             dma((3,)), dma((NS,)), dma((NS,)), dma((2,)), dma((2,)),

time: 61.8 us -> 59.6 us (0.964)
  Pallas kernels: 58.2 us -> 56 us
    pallas_call x1, Pallas kernels: 58.2 us -> 56 us  [window(): pl.pallas_call(kernel, out_shape=(pltpu.VMEM(now.shape, F32), pltpu.VMEM(...]
where the time goes in v4:
time: 59.6 us; the launch traced here: 59.4 us
  Pallas kernels  56 us (94%)
  local copies, waits for them, and re-layouts  2.19 us (4%)
  between operations  1.29 us (2%)
    pallas_call x1, Pallas kernels, window(): pl.pallas_call(kernel, out_shape=(pltpu.VMEM(now.shape, F32), pltpu.VMEM(...  56 us
    unnamed x3, local copies, waits for them, and re-layouts  2.19 us

profile of v4, /device:TPU:0, one launch (start us, length us, event | category | flops | bytes accessed | tf_op | source)
XLA Modules:
  0.0 59.4 jit_solution(6982069827620979660)
XLA Ops:
  1.3 56.0 %shard_map.103 = (f32[1,2,16,32,128]{4,3,2,1,0:T(8,128)S(1)}, f32[1,2,16,32,128]{4,3,2,1,0:T(8,128)S(1)}, f32[2,8,256]{2,1,0:T(8,128)S(1)}) custom-call(f32[16,32,128]{2,1,0:T(8,128)} %tiles.1, s32[16]{0:T(128)} %owner.1, s32[1]{0:T(128)S(6)} %copy.17.offset, f32[1,2,16,32,128]{4,3,2,1,0:T(8,128)} %now.1, f32[1,2,16,32,128]{4,3,2,1,0:T(8,128)} %prev.1, ...), custom_call_target="tpu_custom_call" | custom-call | tf_op jit(solution)/shard_map/pallas_call | solution.py:539
  57.2 0.8 %copy.14 = f32[1,2,16,32,128]{4,3,2,1,0:T(8,128)} copy(f32[1,2,16,32,128]{4,3,2,1,0:T(8,128)S(1)} %get-tuple-element.9) | data formatting | bytes 1048576
  58.0 0.6 %copy.16 = f32[1,2,256,8]{2,3,1,0:T(8,128)} copy(f32[1,2,256,8]{2,3,1,0:T(8,128)S(1)} %bitcast.4) | data formatting | bytes 32768
  58.6 0.8 %copy.15 = f32[1,2,16,32,128]{4,3,2,1,0:T(8,128)} copy(f32[1,2,16,32,128]{4,3,2,1,0:T(8,128)S(1)} %get-tuple-element.10) | data formatting | bytes 1048576

commit v5 on v4

--- a/solution.py
+++ b/solution.py
@@ -19,6 +19,13 @@
 F32 = jnp.float32
 
 
+RING = (0, 1, 2, 1)
+ROW_ORDER = sorted(range(1, GROUP), key=lambda r: -RING[r & 3] - (r >> 3))
+SHOT_ORDER = sorted(
+    range(1, PEERS), key=lambda r: -RING[r >> 3] - RING[(r & 7) >> 1] - 2 * (r & 1)
+)
+
+
 def loop(n, body, start=0):
     lax.fori_loop(start, n, lambda k, c: (body(k), c)[1], 0)
 
@@ -27,9 +34,9 @@
     tiles, owner, offset, now, prev, sources, wavelet, receivers,
     out_now, out_prev, out_traces,
     E0, E1, O, MT, R, SEL, SELH, EDGE, YM, CO, KC, KA, K2, INV, EY,
-    YS, YR, CS, CR, PS, PR, OFS, OFR, OFM, OH, IDL, XB, ACC, TS, TR,
+    YS, YR, CS, CR, PS, PR, OFS, OFR, OFM, OH, IDL, XB, ACC, TS, TR, TX, TY, TG, W,
     in_sem, off_s, off_r, a_sem, b_sem, bh_s, bh_r, e_sem,
-    h_s, h_r, p_s, p_r, t_sem,
+    h_s, h_r, p_s, p_r, t_sem, x_sem, y_sem,
 ):
     s = lax.axis_index("shot")
     i = lax.axis_index("gx")
@@ -81,7 +88,7 @@
     OFR[s] = jnp.full((1, BZ), offset[0], jnp.int32)
 
     cp_mt.wait()
-    for r in range(1, GROUP):
+    for r in ROW_ORDER:
         send(MT.at[me ^ r], R.at[me], a_sem.at[0], a_sem.at[1], member(r)).start()
     R[me] = MT[me]
 
@@ -292,7 +299,7 @@
                     (s ^ (r >> 2), i ^ (r & 3), row),
                 ).start()
 
-    for r in range(1, GROUP):
+    for r in ROW_ORDER:
         send(SEL.at[r], CO.at[X0 + me, inner_y, :], b_sem.at[0], b_sem.at[1], member(r)).start()
 
     @pl.when(tail | head)
@@ -323,52 +330,9 @@
 
     unpack(O, 2, PR)
 
-    all_of(SEL.at[pl.ds(0, GROUP - 1)], b_sem.at[0])
-    all_of(CO.at[pl.ds(0, GROUP - 1), inner_y, :], b_sem.at[1])
-
-    @pl.when(tail | head)
-    def _():
-        for r in range(1, GROUP):
-            @pl.when(bh_ok(r))
-            def _():
-                bh_copy(r).wait_send()
-
-    for slot in range(4):
-        source = GROUP - 2 + slot if slot < 2 else slot - 2
-        plane = X0 - 2 + slot if slot < 2 else X0 + BX + slot - 2
-        edge = has[0] if slot < 2 else has[1]
-
-        @pl.when(edge & (me != source))
-        def _():
-            send(
-                SELH.at[0], CO.at[plane, inner_y, :], bh_s.at[0], bh_r.at[slot],
-                (source >> 2, source & 3, j),
-            ).wait_recv()
-
-    for side, to, back in ((0, has[3], has[2]), (1, has[2], has[3])):
-        @pl.when(to)
-        def _():
-            all_of(EDGE.at[side], e_sem.at[0, side])
-
-        @pl.when(back)
-        def _():
-            all_of(YM.at[side], e_sem.at[1, side])
-            for x in range(BX):
-                CO[X0 + x, pl.ds(Y0 - 2 if side == 0 else Y0 + BY, 2)] = YM[side, x]
-
-    def model_tables(x):
-        for q in range(5):
-            at = pl.ds(Y0 - 4 + 8 * q, 8)
-            speed = CO[x, at]
-            inv = INV[x, at]
-            scaled = speed * speed * inv
-            KC[x, at] = 2.0 * inv - 7.5 * scaled
-            KA[x, at] = (4.0 / 3.0) * scaled
-
-    loop(X0 + BX + 2, model_tables, X0 - 2)
-
     def advance(
-        read, before, write, first, stride, blocks, wide, tiles, step, lift=(0, 0), beside=None
+        read, before, write, first, stride, blocks, wide, tiles, step, lift=(0, 0), beside=None,
+        ahead=False,
     ):
         def planes(block):
             x_first = first + stride * block
@@ -388,7 +352,8 @@
                 ]
                 for k in range(wide):
                     x = x_first + k
-                    kc, ka, k2 = KC[x, at], KA[x, at], K2[x, at]
+                    if not ahead:
+                        kc, ka, k2 = KC[x, at], KA[x, at], K2[x, at]
                     for sh in range(SHOTS):
                         c = line[sh][k]
                         a = (line[sh][k + 1] + line[sh][k - 1]) + (
@@ -405,6 +370,9 @@
                             pltpu.roll(c, 2, 1) * second_lane
                             + pltpu.roll(c, BZ - 2, 1) * last_two
                         )
+                        if ahead:
+                            write[sh, x, at] = a - 0.0625 * b
+                            continue
                         fresh = (kc * c - k2 * before[sh, x, at]) + ka * (a - 0.0625 * b)
                         fresh = fresh + EY[sh, at] * on[k][sh]
                         write[sh, x - lift[0], pl.ds(y - lift[1], 8)] = fresh
@@ -415,6 +383,62 @@
 
     wide_tiles = [Y0 - 4 + 8 * q for q in range(5)]
     own_tiles = [Y0 + 8 * q for q in range(4)]
+
+    advance(E0, O, W, X0 - 2, 4, 5, 4, wide_tiles, 0, ahead=True)
+
+    all_of(SEL.at[pl.ds(0, GROUP - 1)], b_sem.at[0])
+    all_of(CO.at[pl.ds(0, GROUP - 1), inner_y, :], b_sem.at[1])
+
+    @pl.when(tail | head)
+    def _():
+        for r in range(1, GROUP):
+            @pl.when(bh_ok(r))
+            def _():
+                bh_copy(r).wait_send()
+
+    for slot in range(4):
+        source = GROUP - 2 + slot if slot < 2 else slot - 2
+        plane = X0 - 2 + slot if slot < 2 else X0 + BX + slot - 2
+        edge = has[0] if slot < 2 else has[1]
+
+        @pl.when(edge & (me != source))
+        def _():
+            send(
+                SELH.at[0], CO.at[plane, inner_y, :], bh_s.at[0], bh_r.at[slot],
+                (source >> 2, source & 3, j),
+            ).wait_recv()
+
+    for side, to, back in ((0, has[3], has[2]), (1, has[2], has[3])):
+        @pl.when(to)
+        def _():
+            all_of(EDGE.at[side], e_sem.at[0, side])
+
+        @pl.when(back)
+        def _():
+            all_of(YM.at[side], e_sem.at[1, side])
+            for x in range(BX):
+                CO[X0 + x, pl.ds(Y0 - 2 if side == 0 else Y0 + BY, 2)] = YM[side, x]
+
+    def first_step(x):
+        on = [
+            jnp.where(sources[0, sh, 0] == i * BX + x - X0, wavelet[0, sh, 0], 0.0)
+            for sh in range(SHOTS)
+        ]
+        for y in wide_tiles:
+            at = pl.ds(y, 8)
+            speed = CO[x, at]
+            inv = INV[x, at]
+            scaled = speed * speed * inv
+            kc = 2.0 * inv - 7.5 * scaled
+            ka = (4.0 / 3.0) * scaled
+            k2 = K2[x, at]
+            KC[x, at] = kc
+            KA[x, at] = ka
+            for sh in range(SHOTS):
+                fresh = (kc * E0[sh, x, at] - k2 * O[sh, x, at]) + ka * W[sh, x, at]
+                O[sh, x, at] = fresh + EY[sh, at] * on[sh]
+
+    loop(X0 + BX + 2, first_step, X0 - 2)
 
     ends = [wide_tiles[0], wide_tiles[4]]
 
@@ -466,47 +490,62 @@
 
         return some
 
-    def trace_send(pair):
-        for r in range(1, PEERS):
+    def trace_gx(pair):
+        for r in (2, 1, 3):
             send(
-                TS.at[pair], TR.at[pair, mine], t_sem.at[0, pair], t_sem.at[1, pair],
-                (s, i ^ (r >> 3), j ^ (r & 7)),
+                TS.at[pair], TX.at[pair, i], x_sem.at[0, pair], x_sem.at[1, pair], (s, i ^ r, j)
             ).start()
-        TR[pair, mine] = TS[pair]
-
-    def trace_sum(pair):
-        all_of(TR.at[pair, pl.ds(0, PEERS - 1)], t_sem.at[0, pair])
-        all_of(TR.at[pair, pl.ds(0, PEERS - 1)], t_sem.at[1, pair])
-        parts = [TR[pair, q] for q in range(PEERS)]
+        TX[pair, i] = TS[pair]
+
+    def tree(parts):
         while len(parts) > 1:
             parts = [a + b for a, b in zip(parts[0::2], parts[1::2])]
+        return parts[0]
+
+    def trace_gy(pair):
+        all_of(TX.at[pair, pl.ds(0, NX - 1)], x_sem.at[0, pair])
+        all_of(TX.at[pair, pl.ds(0, NX - 1)], x_sem.at[1, pair])
+        TG[pair] = tree([TX[pair, q] for q in range(NX)])
+        for r in range(NY - 1, 0, -1):
+            send(
+                TG.at[pair], TY.at[pair, j], y_sem.at[0, pair], y_sem.at[1, pair], (s, i, j ^ r)
+            ).start()
+        TY[pair, j] = TG[pair]
+
+    def put_traces(pair, total):
         for row in range(8):
             half, sh, part = row // 4, (row // 2) % 2, row % 2
             out_traces[sh, 2 * pair + half : 2 * pair + half + 1, 128 * part : 128 * part + 128] = (
-                parts[0][row : row + 1]
+                total[row : row + 1]
             )
 
+    def trace_out(pair):
+        all_of(TY.at[pair, pl.ds(0, NY - 1)], y_sem.at[0, pair])
+        all_of(TY.at[pair, pl.ds(0, NY - 1)], y_sem.at[1, pair])
+        put_traces(pair, tree([TY[pair, q] for q in range(NY)]))
+
     pairs = STEPS // 2
-    outer_middle(E0, 0)
-    outer_sides(E0, 0)
     for pair in range(pairs):
         even, later = ((E0, E1), (E1, E0))[pair % 2]
         slot = (pair + 1) % 2
         step = 2 * pair + 1
-        outer_ends(even, step - 1)
+        if pair:
+            outer_ends(even, step - 1)
         if pair < pairs - 1:
             advance(O, even, later, X0, 4, 4, 4, [own_tiles[0], own_tiles[3]], step)
+            send_corners(later, slot)
             send_rows(later, slot)
-            send_corners(later, slot)
             advance(O, even, later, X0, 12, 2, 4, own_tiles[1:3], step)
             send_sides(later, slot)
             advance(O, even, later, X0 + 4, 4, 2, 4, own_tiles[1:3], step)
             sample(O, pair, 0)
             sample(later, pair, 1)
-            trace_send(pair)
+            trace_gx(pair)
+            if pair:
+                trace_gy(pair - 1)
             outer_middle(later, step + 1)
-            if pair:
-                trace_sum(pair - 1)
+            if pair > 1:
+                trace_out(pair - 2)
             wait_some(later, slot, range(2))
             outer_sides(later, step + 1)
             wait_rest(later, slot)
@@ -523,10 +562,19 @@
             for sh in range(SHOTS):
                 keep(pair, 0, sh, jnp.sum(ACC[sh], axis=0, keepdims=True))
             sample(final, pair, 1, (0, 0))
-            trace_send(pair)
-            trace_sum(pair - 1)
-            trace_sum(pair)
+            for r in SHOT_ORDER:
+                send(
+                    TS.at[pair], TR.at[mine], t_sem.at[0], t_sem.at[1],
+                    (s, i ^ (r >> 3), j ^ (r & 7)),
+                ).start()
+            TR[mine] = TS[pair]
+            trace_gy(pair - 1)
+            trace_out(pair - 2)
             cp_last.wait()
+            trace_out(pair - 1)
+            all_of(TR.at[pl.ds(0, PEERS - 1)], t_sem.at[0])
+            all_of(TR.at[pl.ds(0, PEERS - 1)], t_sem.at[1])
+            put_traces(pair, tree([TR[q] for q in range(PEERS)]))
 
 
 def window(tiles, owner, offset, now, prev, sources, wavelet, receivers):
@@ -575,10 +623,15 @@
             buf((SHOTS * BX * BY, 2 * BZ), jnp.bfloat16),
             buf((SHOTS, 8, RECS), F32),
             buf((STEPS // 2, 8, 128), F32),
-            buf((STEPS // 2, PEERS, 8, 128), F32),
+            buf((PEERS, 8, 128), F32),
+            buf((STEPS // 2 - 1, NX, 8, 128), F32),
+            buf((STEPS // 2 - 1, NY, 8, 128), F32),
+            buf((STEPS // 2 - 1, 8, 128), F32),
+            buf((SHOTS,) + padded, F32),
             dma((3,)), dma((NS,)), dma((NS,)), dma((2,)), dma((2,)),
             dma((GROUP,)), dma((4,)), dma((2, 2)),
-            dma((2, 8)), dma((2, 8)), dma((4,)), dma((4,)), dma((2, STEPS // 2)),
+            dma((2, 8)), dma((2, 8)), dma((4,)), dma((4,)), dma((2,)),
+            dma((2, STEPS // 2 - 1)), dma((2, STEPS // 2 - 1)),
         ],
         compiler_params=pltpu.CompilerParams(collective_id=0, has_side_effects=True),
     )(tiles, owner, offset, now, prev, sources, wavelet, jnp.transpose(receivers, (2, 0, 1)))

time: 59.6 us -> 55.2 us (0.926)
  Pallas kernels: 56 us -> 51.6 us
    pallas_call x1, Pallas kernels: 56 us -> 51.6 us  [window(): pl.pallas_call(kernel, out_shape=(pltpu.VMEM(now.shape, F32), pltpu.VMEM(...]
where the time goes in v5:
time: 55.2 us; the launch traced here: 55.1 us
  Pallas kernels  51.6 us (93%)
  local copies, waits for them, and re-layouts  2.19 us (4%)
  between operations  1.29 us (2%)
    pallas_call x1, Pallas kernels, window(): pl.pallas_call(kernel, out_shape=(pltpu.VMEM(now.shape, F32), pltpu.VMEM(...  51.6 us
    unnamed x3, local copies, waits for them, and re-layouts  2.19 us

profile of v5, /device:TPU:0, one launch (start us, length us, event | category | flops | bytes accessed | tf_op | source)
XLA Modules:
  0.0 55.1 jit_solution(17981204441275462967)
XLA Ops:
  1.3 51.6 %shard_map.103 = (f32[1,2,16,32,128]{4,3,2,1,0:T(8,128)S(1)}, f32[1,2,16,32,128]{4,3,2,1,0:T(8,128)S(1)}, f32[2,8,256]{2,1,0:T(8,128)S(1)}) custom-call(f32[16,32,128]{2,1,0:T(8,128)} %tiles.1, s32[16]{0:T(128)} %owner.1, s32[1]{0:T(128)S(6)} %copy.17.offset, f32[1,2,16,32,128]{4,3,2,1,0:T(8,128)} %now.1, f32[1,2,16,32,128]{4,3,2,1,0:T(8,128)} %prev.1, ...), custom_call_target="tpu_custom_call" | custom-call | tf_op jit(solution)/shard_map/pallas_call | solution.py:587
  52.9 0.8 %copy.14 = f32[1,2,16,32,128]{4,3,2,1,0:T(8,128)} copy(f32[1,2,16,32,128]{4,3,2,1,0:T(8,128)S(1)} %get-tuple-element.9) | data formatting | bytes 1048576
  53.7 0.6 %copy.16 = f32[1,2,256,8]{2,3,1,0:T(8,128)} copy(f32[1,2,256,8]{2,3,1,0:T(8,128)S(1)} %bitcast.4) | data formatting | bytes 32768
  54.3 0.8 %copy.15 = f32[1,2,16,32,128]{4,3,2,1,0:T(8,128)} copy(f32[1,2,16,32,128]{4,3,2,1,0:T(8,128)S(1)} %get-tuple-element.10) | data formatting | bytes 1048576

commit v6 on v5

--- a/solution.py
+++ b/solution.py
@@ -575,6 +575,17 @@
             all_of(TR.at[pl.ds(0, PEERS - 1)], t_sem.at[0])
             all_of(TR.at[pl.ds(0, PEERS - 1)], t_sem.at[1])
             put_traces(pair, tree([TR[q] for q in range(PEERS)]))
+
+
+def store(a, b, c, to_a, to_b, to_c, sem):
+    copies = [
+        pltpu.make_async_copy(x, y, sem.at[n])
+        for n, (x, y) in enumerate(((a, to_a), (b, to_b), (c, to_c)))
+    ]
+    for copy in copies:
+        copy.start()
+    for copy in copies:
+        copy.wait()
 
 
 def window(tiles, owner, offset, now, prev, sources, wavelet, receivers):
@@ -635,6 +646,18 @@
         ],
         compiler_params=pltpu.CompilerParams(collective_id=0, has_side_effects=True),
     )(tiles, owner, offset, now, prev, sources, wavelet, jnp.transpose(receivers, (2, 0, 1)))
+    hbm = pl.BlockSpec(memory_space=pltpu.HBM)
+    out_now, out_prev, traces = pl.pallas_call(
+        store,
+        out_shape=(
+            jax.ShapeDtypeStruct(now.shape, F32),
+            jax.ShapeDtypeStruct(prev.shape, F32),
+            jax.ShapeDtypeStruct((SHOTS, STEPS, RECS), F32),
+        ),
+        in_specs=[any_spec] * 3,
+        out_specs=(hbm, hbm, hbm),
+        scratch_shapes=[dma((3,))],
+    )(*[pltpu.with_memory_space_constraint(x, pltpu.VMEM) for x in (out_now, out_prev, traces)])
     return out_now, out_prev, jnp.transpose(traces, (0, 2, 1))[None]
 
 

time: 55.2 us -> 54 us (0.978)
  local copies, waits for them, and re-layouts: 2.19 us -> 0 us
  Pallas kernels: 51.6 us -> 52.6 us
    unnamed x3 -> x0, local copies, waits for them, and re-layouts: 2.19 us -> none
    pallas_call x0 -> x1, Pallas kernels: none -> 1 us  [window(): pl.pallas_call(store, out_shape=(jax.ShapeDtypeStruct(now.shape, F32), ja...]
where the time goes in v6:
time: 54 us; the launch traced here: 53.9 us
  Pallas kernels  52.6 us (97%)
  between operations  1.29 us (2%)
    pallas_call x1, Pallas kernels, window(): pl.pallas_call(kernel, out_shape=(pltpu.VMEM(now.shape, F32), pltpu.VMEM(...  51.6 us

profile of v6, /device:TPU:0, one launch (start us, length us, event | category | flops | bytes accessed | tf_op | source)
XLA Modules:
  0.0 53.9 jit_solution(15558695677233588417)
XLA Ops:
  1.3 51.6 %shard_map.103 = (f32[1,2,16,32,128]{4,3,2,1,0:T(8,128)S(1)}, f32[1,2,16,32,128]{4,3,2,1,0:T(8,128)S(1)}, f32[2,8,256]{2,1,0:T(8,128)S(1)}) custom-call(f32[16,32,128]{2,1,0:T(8,128)} %tiles.1, s32[16]{0:T(128)} %owner.1, s32[1]{0:T(128)S(6)} %copy.11.offset, f32[1,2,16,32,128]{4,3,2,1,0:T(8,128)} %now.1, f32[1,2,16,32,128]{4,3,2,1,0:T(8,128)} %prev.1, ...), custom_call_target="tpu_custom_call" | custom-call | tf_op jit(solution)/shard_map/pallas_call | solution.py:598
  52.9 1.0 %shard_map.104 = (f32[1,2,16,32,128]{4,3,2,1,0:T(8,128)}, f32[1,2,16,32,128]{4,3,2,1,0:T(8,128)}, f32[2,8,256]{2,1,0:T(8,128)}) custom-call(f32[1,2,16,32,128]{4,3,2,1,0:T(8,128)S(1)} %get-tuple-element.9.a, f32[1,2,16,32,128]{4,3,2,1,0:T(8,128)S(1)} %get-tuple-element.10.b, f32[2,8,256]{2,1,0:T(8,128)S(1)} %get-tuple-element.11.c), custom_call_target="tpu_custom_call" | custom-call | tf_op jit(solution)/shard_map/pallas_call | solution.py:650

commit v7 on v6

--- a/solution.py
+++ b/solution.py
@@ -16,6 +16,7 @@
 PX, PY = BX + 8, BY + 16
 X0, Y0 = 4, 8
 MESH = pl.DeviceIdType.MESH
+MATMUL_SHOTS = (1,)
 F32 = jnp.float32
 
 
@@ -34,7 +35,7 @@
     tiles, owner, offset, now, prev, sources, wavelet, receivers,
     out_now, out_prev, out_traces,
     E0, E1, O, MT, R, SEL, SELH, EDGE, YM, CO, KC, KA, K2, INV, EY,
-    YS, YR, CS, CR, PS, PR, OFS, OFR, OFM, OH, IDL, XB, ACC, TS, TR, TX, TY, TG, W,
+    YS, YR, CS, CR, PS, PR, OFS, OFR, OFM, OH, IDL, XB, ACC, TS, TR, TX, TY, TG, W, BAND,
     in_sem, off_s, off_r, a_sem, b_sem, bh_s, bh_r, e_sem,
     h_s, h_r, p_s, p_r, t_sem, x_sem, y_sem,
 ):
@@ -227,6 +228,12 @@
             inv = 1.0 / (1.0 + 0.3 * (wx * wx + wy * wy))
             hit = (cells == sources[0, sh, 1]) & (lanes == sources[0, sh, 2])
             EY[sh, pl.ds(Y0 - 4 + 8 * q, 8)] = jnp.where(hit, inv, 0.0)
+
+    gap = jnp.abs(
+        (lax.broadcasted_iota(jnp.int32, (2 * BZ, BZ), 0) & (BZ - 1))
+        - lax.broadcasted_iota(jnp.int32, (2 * BZ, BZ), 1)
+    )
+    BAND[...] = jnp.where(gap == 1, 1.0, jnp.where(gap == 2, -0.0625, 0.0)).astype(jnp.bfloat16)
 
     rx = receivers[0] - i * BX
     ry = receivers[1] - j * BY
@@ -345,11 +352,24 @@
                 ]
                 for k in range(wide)
             ]
-            for y in tiles:
+            lines = [
+                [
+                    {d: read[sh, x_first + d, pl.ds(y, 8)] for d in range(-2, wide + 2)}
+                    for sh in range(SHOTS)
+                ]
+                for y in tiles
+            ]
+            deep = {}
+            for sh in MATMUL_SHOTS:
+                v = jnp.concatenate([ln[sh][k] for ln in lines for k in range(wide)], axis=0)
+                high = v.astype(jnp.bfloat16)
+                low = (v - high.astype(F32)).astype(jnp.bfloat16)
+                deep[sh] = jnp.dot(
+                    jnp.concatenate([high, low], axis=1), BAND[...], preferred_element_type=F32
+                )
+            for n, y in enumerate(tiles):
                 at = pl.ds(y, 8)
-                line = [
-                    {d: read[sh, x_first + d, at] for d in range(-2, wide + 2)} for sh in range(SHOTS)
-                ]
+                line = lines[n]
                 for k in range(wide):
                     x = x_first + k
                     if not ahead:
@@ -362,18 +382,23 @@
                         b = (line[sh][k + 2] + line[sh][k - 2]) + (
                             read[sh, x, pl.ds(y + 2, 8)] + read[sh, x, pl.ds(y - 2, 8)]
                         )
-                        a = a + (
-                            pltpu.roll(c, 1, 1) * first_lane
-                            + pltpu.roll(c, BZ - 1, 1) * last_lane
-                        )
-                        b = b + (
-                            pltpu.roll(c, 2, 1) * second_lane
-                            + pltpu.roll(c, BZ - 2, 1) * last_two
-                        )
+                        if sh in deep:
+                            m = 8 * (n * wide + k)
+                            near = (a - 0.0625 * b) + deep[sh][m : m + 8]
+                        else:
+                            a = a + (
+                                pltpu.roll(c, 1, 1) * first_lane
+                                + pltpu.roll(c, BZ - 1, 1) * last_lane
+                            )
+                            b = b + (
+                                pltpu.roll(c, 2, 1) * second_lane
+                                + pltpu.roll(c, BZ - 2, 1) * last_two
+                            )
+                            near = a - 0.0625 * b
                         if ahead:
-                            write[sh, x, at] = a - 0.0625 * b
+                            write[sh, x, at] = near
                             continue
-                        fresh = (kc * c - k2 * before[sh, x, at]) + ka * (a - 0.0625 * b)
+                        fresh = (kc * c - k2 * before[sh, x, at]) + ka * near
                         fresh = fresh + EY[sh, at] * on[k][sh]
                         write[sh, x - lift[0], pl.ds(y - lift[1], 8)] = fresh
             if beside is not None:
@@ -449,7 +474,7 @@
         advance(even, O, O, X0 - 2, BX, 2, 4, wide_tiles[1:4], step)
 
     def outer_ends(even, step):
-        advance(even, O, O, X0 - 2, 4, 5, 4, ends, step)
+        advance(even, O, O, X0 - 2, 20, 1, 20, ends, step)
 
     row_ids = lax.broadcasted_iota(jnp.int32, (BX * BY, RECS), 0)
 
@@ -532,7 +557,7 @@
         if pair:
             outer_ends(even, step - 1)
         if pair < pairs - 1:
-            advance(O, even, later, X0, 4, 4, 4, [own_tiles[0], own_tiles[3]], step)
+            advance(O, even, later, X0, 16, 1, 16, [own_tiles[0], own_tiles[3]], step)
             send_corners(later, slot)
             send_rows(later, slot)
             advance(O, even, later, X0, 12, 2, 4, own_tiles[1:3], step)
@@ -639,6 +664,7 @@
             buf((STEPS // 2 - 1, NY, 8, 128), F32),
             buf((STEPS // 2 - 1, 8, 128), F32),
             buf((SHOTS,) + padded, F32),
+            buf((2 * BZ, BZ), jnp.bfloat16),
             dma((3,)), dma((NS,)), dma((NS,)), dma((2,)), dma((2,)),
             dma((GROUP,)), dma((4,)), dma((2, 2)),
             dma((2, 8)), dma((2, 8)), dma((4,)), dma((4,)), dma((2,)),

time: 54 us -> 52 us (0.963)
  Pallas kernels: 52.6 us -> 50.6 us
    pallas_call x1, Pallas kernels: 51.6 us -> 49.6 us  [window(): pl.pallas_call(kernel, out_shape=(pltpu.VMEM(now.shape, F32), pltpu.VMEM(...]
where the time goes in v7:
time: 52 us; the launch traced here: 51.9 us
  Pallas kernels  50.6 us (97%)
  between operations  1.29 us (2%)
    pallas_call x1, Pallas kernels, window(): pl.pallas_call(kernel, out_shape=(pltpu.VMEM(now.shape, F32), pltpu.VMEM(...  49.6 us

profile of v7, /device:TPU:0, one launch (start us, length us, event | category | flops | bytes accessed | tf_op | source)
XLA Modules:
  0.0 51.9 jit_solution(158064045782317850)
XLA Ops:
  1.3 49.6 %shard_map.103 = (f32[1,2,16,32,128]{4,3,2,1,0:T(8,128)S(1)}, f32[1,2,16,32,128]{4,3,2,1,0:T(8,128)S(1)}, f32[2,8,256]{2,1,0:T(8,128)S(1)}) custom-call(f32[16,32,128]{2,1,0:T(8,128)} %tiles.1, s32[16]{0:T(128)} %owner.1, s32[1]{0:T(128)S(6)} %copy.11.offset, f32[1,2,16,32,128]{4,3,2,1,0:T(8,128)} %now.1, f32[1,2,16,32,128]{4,3,2,1,0:T(8,128)} %prev.1, ...), custom_call_target="tpu_custom_call" | custom-call | tf_op jit(solution)/shard_map/pallas_call | solution.py:623
  50.9 1.0 %shard_map.104 = (f32[1,2,16,32,128]{4,3,2,1,0:T(8,128)}, f32[1,2,16,32,128]{4,3,2,1,0:T(8,128)}, f32[2,8,256]{2,1,0:T(8,128)}) custom-call(f32[1,2,16,32,128]{4,3,2,1,0:T(8,128)S(1)} %get-tuple-element.9.a, f32[1,2,16,32,128]{4,3,2,1,0:T(8,128)S(1)} %get-tuple-element.10.b, f32[2,8,256]{2,1,0:T(8,128)S(1)} %get-tuple-element.11.c), custom_call_target="tpu_custom_call" | custom-call | tf_op jit(solution)/shard_map/pallas_call | solution.py:676

commit v8 on v7

--- a/solution.py
+++ b/solution.py
@@ -16,7 +16,7 @@
 PX, PY = BX + 8, BY + 16
 X0, Y0 = 4, 8
 MESH = pl.DeviceIdType.MESH
-MATMUL_SHOTS = (1,)
+MATMUL_SHOTS = (0, 1)
 F32 = jnp.float32
 
 
@@ -409,7 +409,7 @@
     wide_tiles = [Y0 - 4 + 8 * q for q in range(5)]
     own_tiles = [Y0 + 8 * q for q in range(4)]
 
-    advance(E0, O, W, X0 - 2, 4, 5, 4, wide_tiles, 0, ahead=True)
+    advance(E0, O, W, X0 - 2, 10, 2, 10, wide_tiles, 0, ahead=True)
 
     all_of(SEL.at[pl.ds(0, GROUP - 1)], b_sem.at[0])
     all_of(CO.at[pl.ds(0, GROUP - 1), inner_y, :], b_sem.at[1])
@@ -504,7 +504,7 @@
             keep(pair, half, sh, got)
 
     def sample_beside(buf):
-        def some(block):
+        def four(block):
             split(buf, block, (X0, Y0))
             wanted = IDL[...] - 4 * BY * block
             for sh in range(SHOTS):
@@ -512,6 +512,10 @@
                 picked = jnp.dot(XB[at], OH[...], preferred_element_type=F32)
                 hit = jnp.where(row_ids[: 4 * BY] == wanted, picked, 0.0)
                 ACC[sh] += jnp.sum(hit.reshape(4 * BY // 8, 8, RECS), axis=0)
+
+        def some(block):
+            four(2 * block)
+            four(2 * block + 1)
 
         return some
 
@@ -582,7 +586,7 @@
             final = out_now.at[0]
             ACC[...] = jnp.zeros_like(ACC)
             advance(
-                O, even, final, X0, 4, 4, 4, own_tiles, step, (X0, Y0), sample_beside(O)
+                O, even, final, X0, 8, 2, 8, own_tiles, step, (X0, Y0), sample_beside(O)
             )
             for sh in range(SHOTS):
                 keep(pair, 0, sh, jnp.sum(ACC[sh], axis=0, keepdims=True))

time: 52 us -> 51.9 us (level)
  no operation moved by 1% of the time
where the time goes in v8:
time: 51.9 us; the launch traced here: 51.7 us
  Pallas kernels  50.5 us (97%)
  between operations  1.29 us (2%)
    pallas_call x1, Pallas kernels, window(): pl.pallas_call(kernel, out_shape=(pltpu.VMEM(now.shape, F32), pltpu.VMEM(...  49.5 us

profile of v8, /device:TPU:0, one launch (start us, length us, event | category | flops | bytes accessed | tf_op | source)
XLA Modules:
  0.0 51.7 jit_solution(6618664876372682145)
XLA Ops:
  1.3 49.5 %shard_map.103 = (f32[1,2,16,32,128]{4,3,2,1,0:T(8,128)S(1)}, f32[1,2,16,32,128]{4,3,2,1,0:T(8,128)S(1)}, f32[2,8,256]{2,1,0:T(8,128)S(1)}) custom-call(f32[16,32,128]{2,1,0:T(8,128)} %tiles.1, s32[16]{0:T(128)} %owner.1, s32[1]{0:T(128)S(6)} %copy.11.offset, f32[1,2,16,32,128]{4,3,2,1,0:T(8,128)} %now.1, f32[1,2,16,32,128]{4,3,2,1,0:T(8,128)} %prev.1, ...), custom_call_target="tpu_custom_call" | custom-call | tf_op jit(solution)/shard_map/pallas_call | solution.py:627
  50.7 1.0 %shard_map.104 = (f32[1,2,16,32,128]{4,3,2,1,0:T(8,128)}, f32[1,2,16,32,128]{4,3,2,1,0:T(8,128)}, f32[2,8,256]{2,1,0:T(8,128)}) custom-call(f32[1,2,16,32,128]{4,3,2,1,0:T(8,128)S(1)} %get-tuple-element.9.a, f32[1,2,16,32,128]{4,3,2,1,0:T(8,128)S(1)} %get-tuple-element.10.b, f32[2,8,256]{2,1,0:T(8,128)S(1)} %get-tuple-element.11.c), custom_call_target="tpu_custom_call" | custom-call | tf_op jit(solution)/shard_map/pallas_call | solution.py:680
